TPU v7x, 32 devices: a whole 2x2x4 slice. The times are simulated.
32 devices in a mesh: px: 4 (over z), py: 8 (over y, x, core).
Axes of the slice: x: 2, y: 2, z: 4, core: 2. Of those that a mesh axis runs over, the one named last changes fastest.
Arguments:
- vorticity: float32 [3, 192, 36864], P(None, 'px', 'py'), may hold values from -6 to 6
Outputs:
- velocity: float32 [3, 192, 36864], P(None, 'px', 'py')
- stretching: float32 [3, 192, 36864], P(None, 'px', 'py')
All inputs are finite; a program needn't handle non-finite values.
Results may differ from a plain program's by a relative error of at most 0.0003.
Values sent between devices are 32-bit elements; how exact they have to be, the bound alone decides.
No kernel may reach another device: no remote copies, remote signals or barrier semaphores. Data moves between devices by JAX's collectives and lax.ppermute only.
A program may use at most 128 MiB of HBM per device.

v0:
```python
import math

import jax
import jax.numpy as jnp
from jax import lax
from jax.sharding import PartitionSpec as P

G = 192


smoothing = 1.0
highest = lax.Precision.HIGHEST


def with_halo(shard, sides, width):
    for axis, dim in sides:
        devices, length = (lax.axis_size(axis), shard.shape[dim])
        up = [(i, (i + 1) % devices) for i in range(devices - 1)]
        down = [(j, i) for i, j in up]
        last = lax.slice_in_dim(shard, length - width, length, axis=dim)
        leading = lax.slice_in_dim(shard, 0, width, axis=dim)
        before = lax.ppermute(last, axis, up)
        after = lax.ppermute(leading, axis, down)
        shard = jnp.concatenate([before, shard, after], axis=dim)
    return shard


def twiddle(count_in, count_out, length, factor):
    source = lax.broadcasted_iota(jnp.int32, (count_in, count_out), 0)
    target = lax.broadcasted_iota(jnp.int32, (count_in, count_out), 1)
    angle = (source * target % length).astype(jnp.float32) * (2.0 * math.pi / length)
    cosine = jnp.cos(angle) * factor
    sine = jnp.sin(angle) * factor
    return (
        jnp.broadcast_to(cosine, (3, count_in, count_out)),
        jnp.broadcast_to(sine, (3, count_in, count_out)),
    )


def product(einsum_form, first, second):
    return jnp.einsum(einsum_form, first, second, precision=highest)


def forward_left(pair, einsum_form, tables):
    real_part, imag_part = pair
    cosine_table, sine_table = tables
    return (
        product(einsum_form, cosine_table, real_part) + product(einsum_form, sine_table, imag_part),
        product(einsum_form, cosine_table, imag_part) - product(einsum_form, sine_table, real_part),
    )


def forward_right(pair, einsum_form, tables):
    real_part, imag_part = pair
    cosine_table, sine_table = tables
    return (
        product(einsum_form, real_part, cosine_table) + product(einsum_form, imag_part, sine_table),
        product(einsum_form, imag_part, cosine_table) - product(einsum_form, real_part, sine_table),
    )


def backward_left(pair, einsum_form, tables):
    real_part, imag_part = pair
    cosine_table, sine_table = tables
    return (
        product(einsum_form, cosine_table, real_part) - product(einsum_form, sine_table, imag_part),
        product(einsum_form, cosine_table, imag_part) + product(einsum_form, sine_table, real_part),
    )


def wavenumbers(start, count, length, position):
    index = start + lax.iota(jnp.int32, count)
    signed = jnp.where(index < length // 2, index, index - length)
    wave = signed.astype(jnp.float32) * (2.0 * math.pi / length)
    slope = jnp.where(index == length // 2, 0.0, wave)
    keep = jnp.where(index == length // 2, 0.0, 1.0)
    shape = [1, 1, 1, 1]
    shape[position] = count
    return (wave.reshape(shape), slope.reshape(shape), keep.reshape(shape))


def velocity_spectrum(pair, waves_x, waves_y, waves_z):
    square = waves_x[0] ** 2 + waves_y[0] ** 2 + waves_z[0] ** 2
    mask = waves_x[2] * waves_y[2] * waves_z[2]
    green = (
        mask
        * jnp.exp(-0.5 * smoothing * smoothing * square)
        / (square + jnp.where(square == 0.0, 1.0, 0.0))
    )
    slope_x, slope_y, slope_z = (waves_x[1][0], waves_y[1][0], waves_z[1][0])

    def curl(field):
        return jnp.stack(
            [
                slope_y * field[2] - slope_z * field[1],
                slope_z * field[0] - slope_x * field[2],
                slope_x * field[1] - slope_y * field[0],
            ]
        )

    real_part = pair[0] * green
    imag_part = pair[1] * green
    return (jnp.swapaxes(-curl(imag_part), 1, 2), jnp.swapaxes(curl(real_part), 1, 2))


def window(padded, axis, offset):
    starts = [0, 2, 2, 2]
    limits = [padded.shape[0], padded.shape[1] - 2, padded.shape[2] - 2, padded.shape[3] - 2]
    starts[axis] = starts[axis] + offset
    limits[axis] = limits[axis] + offset
    return lax.slice(padded, starts, limits)


def derivative(padded, axis):
    near = window(padded, axis, 1) - window(padded, axis, -1)
    far = window(padded, axis, 2) - window(padded, axis, -2)
    return (8.0 * near - far) / 12.0


def on_device(vorticity):
    block_rows = vorticity.shape[1]
    block_cols = vorticity.shape[2] // G
    field = vorticity.reshape(3, block_rows, block_cols, G)
    length = 2 * G
    depth_tables = twiddle(G, G, length, 1.0)
    line_tables = twiddle(G, length, length, 1.0)
    inverse_tables = twiddle(length, G, length, 1.0 / length)
    closing = twiddle(G, G, length, 1.0 / length)
    weights = jnp.where(lax.iota(jnp.int32, G) == 0, 1.0, 2.0)[None, :, None]
    closing_cos = closing[0] * weights
    closing_sin = closing[1] * weights
    pair = (
        product("czk,cxyz->ckxy", depth_tables[0], field),
        -product("czk,cxyz->ckxy", depth_tables[1], field),
    )
    pair = (
        lax.all_to_all(pair[0], "py", split_axis=1, concat_axis=3, tiled=True),
        lax.all_to_all(pair[1], "py", split_axis=1, concat_axis=3, tiled=True),
    )
    pair = forward_left(pair, "cyl,ckxy->clkx", line_tables)
    pair = (
        lax.all_to_all(pair[0], "px", split_axis=1, concat_axis=3, tiled=True),
        lax.all_to_all(pair[1], "px", split_axis=1, concat_axis=3, tiled=True),
    )
    pair = forward_right(pair, "clkx,cxm->clkm", line_tables)
    rows = pair[0].shape[1]
    depth = pair[0].shape[2]
    waves_y = wavenumbers(lax.axis_index("px") * rows, rows, length, 1)
    waves_z = wavenumbers(lax.axis_index("py") * depth, depth, length, 2)
    waves_x = wavenumbers(0, length, length, 3)
    pair = velocity_spectrum(pair, waves_x, waves_y, waves_z)
    pair = backward_left(pair, "cmx,cklm->cxkl", inverse_tables)
    pair = (
        lax.all_to_all(pair[0], "px", split_axis=1, concat_axis=3, tiled=True),
        lax.all_to_all(pair[1], "px", split_axis=1, concat_axis=3, tiled=True),
    )
    pair = backward_left(pair, "cly,cxkl->cyxk", inverse_tables)
    pair = (
        lax.all_to_all(pair[0], "py", split_axis=1, concat_axis=3, tiled=True),
        lax.all_to_all(pair[1], "py", split_axis=1, concat_axis=3, tiled=True),
    )
    flow = product("cyxk,ckz->cyxz", pair[0], closing_cos) - product(
        "cyxk,ckz->cyxz", pair[1], closing_sin
    )
    flow = jnp.swapaxes(flow, 1, 2)
    padded = with_halo(flow, (("px", 1), ("py", 2)), 2)
    padded = jnp.pad(padded, ((0, 0), (0, 0), (0, 0), (2, 2)))
    stretching = (
        field[0] * derivative(padded, 1)
        + field[1] * derivative(padded, 2)
        + field[2] * derivative(padded, 3)
    )
    return (
        flow.reshape(3, block_rows, block_cols * G),
        stretching.reshape(3, block_rows, block_cols * G),
    )


def solution(mesh):
    in_specs = (P(None, "px", "py"),)
    out_specs = (P(None, "px", "py"), P(None, "px", "py"))
    return jax.shard_map(
        on_device, mesh=mesh, in_specs=in_specs, out_specs=out_specs, check_vma=False
    )
```

profile of v0, /device:TPU:0, one launch (start us, length us, event | category | flops | bytes accessed | tf_op | source)
XLA Modules:
  0.0 1188.7 jit_solution(7702247980146998489)
XLA Ops:
  137.3 14.4 %convolution_add_fusion = f32[3,384,24,48]{1,3,2,0:T(8,128)} fusion(f32[3,384,24,48]{1,3,2,0:T(8,128)S(1)} %fusion.50, f32[3,24,48,192]{2,3,1,0:T(8,128)S(1)} %bitcast.132, f32[192,384]{1,0:T(8,128)S(1)} %fusion.106), kind=kOutput, calls=%fused_computation.68 | convolution fusion | flops 3058974720 | bytes 13565952 | tf_op jit(solution)/shard_map/cyl,ckxy->clkx/dot_general | solution.py:41
  162.7 16.7 %reshape.225 = f32[4,1,331776]{2,1,0:T(1,128)} reshape(f32[384,3,24,48]{3,2,1,0:T(8,128)} %bitcast.136) | data formatting | bytes 10616832
  185.3 14.7 %fusion.54 = f32[3,384,24,48]{1,3,2,0:T(8,128)S(1)} fusion(f32[3,24,48,192]{2,3,1,0:T(8,128)} %bitcast.133, f32[192,384]{1,0:T(8,128)S(1)} %fusion.107), kind=kOutput, calls=%fused_computation.86 | convolution fusion | flops 3057647616 | bytes 8257536 | tf_op jit(solution)/shard_map/cyl,ckxy->clkx/dot_general | solution.py:41
  200.1 14.0 %convolution_subtract_fusion = f32[3,384,24,48]{1,3,2,0:T(8,128)} fusion(f32[3,384,24,48]{1,3,2,0:T(8,128)S(1)} %fusion.54, f32[3,24,48,192]{2,3,1,0:T(8,128)S(1)} %bitcast.131, f32[192,384]{1,0:T(8,128)S(1)} %fusion.106), kind=kOutput, calls=%fused_computation.69 | convolution fusion | flops 3058974720 | bytes 13565952 | tf_op jit(solution)/shard_map/cyl,ckxy->clkx/dot_general | solution.py:41
  225.0 16.9 %reshape.227 = f32[4,1,331776]{2,1,0:T(1,128)} reshape(f32[384,3,24,48]{3,2,1,0:T(8,128)} %bitcast.137) | data formatting | bytes 10616832
  241.9 58.1 %all-to-all-done.3 = f32[4,1,331776]{2,1,0:T(1,128)} async-done(((f32[4,1,331776]{2,1,0:T(1,128)}), f32[4,1,331776]{2,1,0:T(1,128)}, u32[]{:S(2)}, u32[]{:S(2)}) %all-to-all-start.3) | async-done | bytes 5308448 | tf_op jit(solution)/shard_map/all_to_all | solution.py:142
  310.4 53.4 %reduce.3 = f32[4,331776]{1,0:T(4,128)} reduce(f32[4,1,331776]{2,1,0:T(1,128)} %all-to-all-done.3, f32[]{:T(128)} %broadcast.475), dimensions={1}, to_apply=%all_to_all.116.reduce_sub_computation | reduce | bytes 10616836 | tf_op jit(solution)/shard_map/all_to_all | solution.py:142
  363.8 14.1 %reshape.226 = f32[384,3,24,48]{3,2,1,0:T(8,128)} reshape(f32[4,331776]{1,0:T(4,128)} %reduce.3) | data formatting | bytes 10616832
  377.9 12.6 %copy.152 = f32[3,4,96,24,48]{2,1,4,3,0:T(4,128)} copy(f32[3,4,96,24,48]{4,3,0,2,1:T(8,128)} %bitcast.138) | data formatting | bytes 10616832 | tf_op jit(solution)/shard_map/all_to_all | solution.py:142
  406.0 15.4 %fusion.48 = f32[3,96,24,384]{3,2,1,0:T(8,128)} fusion(f32[3,96,24,192]{3,2,1,0:T(8,128)} %copy.111, f32[192,384]{1,0:T(8,128)} %copy-done.5), kind=kOutput, calls=%fused_computation.80 | convolution fusion | flops 6115295232 | bytes 16220160 | tf_op jit(solution)/shard_map/clkx,cxm->clkm/dot_general | solution.py:41
  421.6 53.2 %reduce.2 = f32[4,331776]{1,0:T(4,128)} reduce(f32[4,1,331776]{2,1,0:T(1,128)} %all-to-all-done.2, f32[]{:T(128)} %broadcast.475), dimensions={1}, to_apply=%all_to_all.112.reduce_sub_computation | reduce | bytes 10616836 | tf_op jit(solution)/shard_map/all_to_all | solution.py:143
  474.8 14.0 %reshape.228 = f32[384,3,24,48]{3,2,1,0:T(8,128)} reshape(f32[4,331776]{1,0:T(4,128)} %reduce.2) | data formatting | bytes 10616832
  488.9 12.6 %copy.151 = f32[3,4,96,24,48]{2,1,4,3,0:T(4,128)} copy(f32[3,4,96,24,48]{4,3,0,2,1:T(8,128)} %bitcast.139) | data formatting | bytes 10616832 | tf_op jit(solution)/shard_map/all_to_all | solution.py:143
  517.0 15.8 %fusion.52 = f32[3,96,24,384]{3,2,1,0:T(8,128)} fusion(f32[3,96,24,192]{3,2,1,0:T(8,128)} %copy.105, f32[192,384]{1,0:T(8,128)} %copy-done.5), kind=kOutput, calls=%fused_computation.84 | convolution fusion | flops 6115295232 | bytes 16220160 | tf_op jit(solution)/shard_map/clkx,cxm->clkm/dot_general | solution.py:41
  532.8 16.1 %add_multiply_fusion = f32[3,96,24,384]{3,2,1,0:T(8,128)} fusion(f32[3,96,24,384]{3,2,1,0:T(8,128)} %fusion.48, f32[96,24,384]{2,1,0:T(8,128)S(1)} %fusion.20, f32[3,96,24,192]{3,2,1,0:T(8,128)S(1)} %copy-done.4, f32[192,384]{1,0:T(8,128)} %copy-done.8), kind=kOutput, calls=%fused_computation.3 | convolution fusion | flops 6120603648 | bytes 30375936 | tf_op jit(solution)/shard_map/clkx,cxm->clkm/dot_general | solution.py:41
  549.0 16.0 %subtract_multiply_fusion = f32[3,96,24,384]{3,2,1,0:T(8,128)} fusion(f32[3,96,24,384]{3,2,1,0:T(8,128)} %fusion.52, f32[96,24,384]{2,1,0:T(8,128)S(1)} %fusion.20, f32[3,96,24,192]{3,2,1,0:T(8,128)S(1)} %bitcast.135, f32[192,384]{1,0:T(8,128)} %copy-done.8), kind=kOutput, calls=%fused_computation.4 | convolution fusion | flops 6120603648 | bytes 30375936 | tf_op jit(solution)/shard_map/clkx,cxm->clkm/dot_general | solution.py:41
  564.9 15.2 %multiply_subtract_fusion.4 = (f32[1,96,24,384]{3,2,1,0:T(8,128)}, f32[1,96,24,384]{3,2,1,0:T(8,128)}, f32[1,96,24,384]{3,2,1,0:T(8,128)}, f32[1,96,24,384]{3,2,...) fusion(f32[3,96,24,384]{3,2,1,0:T(8,128)} %subtract_multiply_fusion, f32[384]{0:T(512)S(1)} %fusion.121, ...), kind=kLoop, calls=%fused_computation.60 | loop fusion | flops 15925248 | bytes 42469344 | tf_op jit(solution)/shard_map/sub | solution.py:96
  585.0 17.8 %fusion.3 = f32[3,192,24,96]{3,1,2,0:T(8,128)} fusion(f32[3,24,96,384]{3,1,2,0:T(8,128)S(1)} %maximum_bitcast_fusion, f32[384,192]{0,1:T(8,128)S(1)} %copy-done.7), kind=kOutput, calls=%fused_computation.7 | convolution fusion | flops 6115295232 | bytes 16220160 | tf_op jit(solution)/shard_map/cmx,cklm->cxkl/dot_general | solution.py:41
  607.6 21.8 %fusion.32 = f32[3,192,24,96]{3,1,2,0:T(8,128)S(1)} fusion(f32[3,192,24,96]{3,1,2,0:T(8,128)} %fusion.3, f32[3,24,96,384]{3,1,2,0:T(8,128)S(1)} %fusion, f32[384,192]{0,1:T(8,128)S(1)} %copy-done.6), kind=kOutput, calls=%fused_computation.66 | convolution fusion | flops 6116622336 | bytes 21528576 | tf_op jit(solution)/shard_map/cmx,cklm->cxkl/dot_general | solution.py:41
  641.8 19.6 %fusion.1 = f32[3,192,24,96]{3,1,2,0:T(8,128)S(1)} fusion(f32[3,24,96,384]{3,1,2,0:T(8,128)} %copy-done, f32[384,192]{0,1:T(8,128)S(1)} %copy-done.6), kind=kOutput, calls=%fused_computation.5 | convolution fusion | flops 6115295232 | bytes 16220160 | tf_op jit(solution)/shard_map/cmx,cklm->cxkl/dot_general | solution.py:41
  661.4 15.7 %fusion.35 = f32[3,192,24,96]{3,1,2,0:T(8,128)S(1)} fusion(f32[3,192,24,96]{3,1,2,0:T(8,128)S(1)} %fusion.1, f32[3,24,96,384]{3,1,2,0:T(8,128)S(1)} %copy-done.2, f32[384,192]{0,1:T(8,128)S(1)} %copy-done.7), kind=kOutput, calls=%fused_computation.67 | convolution fusion | flops 6116622336 | bytes 21528576 | tf_op jit(solution)/shard_map/cmx,cklm->cxkl/dot_general | solution.py:41
  684.0 112.3 %all-to-all-done.4 = f32[3,192,24,96]{3,2,0,1:T(8,128)} async-done(((f32[3,192,24,96]{3,2,0,1:T(8,128)}), f32[3,192,24,96]{3,2,0,1:T(8,128)}, u32[]{:S(2)}, u32[]{:S(2)}) %all-to-all-start.4) | async-done | bytes 5308448 | tf_op jit(solution)/shard_map/all_to_all | solution.py:154
  830.0 126.7 %all-to-all-done.5 = f32[3,192,24,96]{3,2,0,1:T(8,128)} async-done(((f32[3,192,24,96]{3,2,0,1:T(8,128)}), f32[3,192,24,96]{3,2,0,1:T(8,128)}, u32[]{:S(2)}, u32[]{:S(2)}) %all-to-all-start.5) | async-done | bytes 5308448 | tf_op jit(solution)/shard_map/all_to_all | solution.py:155
  1110.8 14.0 %subtract_bitcast_fusion = f32[3,48,24,192]{3,1,2,0:T(8,128)S(1)} fusion(f32[3,24,48,192]{3,2,1,0:T(8,128)S(1)} %fusion.72, f32[3,24,48,192]{2,3,1,0:T(8,128)} %bitcast.142, f32[192,192]{1,0:T(8,128)S(1)} %copy-done.14, f32[192]{0:T(256)S(1)} %compare_select_fusion.3), kind=kOutput, calls=%fused_computation.55 | convolution fusion | flops 1529597952 | bytes 8110848 | tf_op jit(solution)/shard_map/cyxk,ckz->cyxz/dot_general | solution.py:41
  (150 shorter events, 486.3 us)
Async XLA Ops:
  29.1 38.2 %all-to-all-start.1 = ((f32[8,1,82944]{2,1,0:T(1,128)}), f32[8,1,82944]{2,1,0:T(1,128)}, u32[]{:S(2)}, u32[]{:S(2)}) async-start(f32[8,1,82944]{2,1,0:T(1,128)} %reshape.221), calls=%async_computation.1 | async-start | bytes 5308416 | tf_op jit(solution)/shard_map/all_to_all | solution.py:137
  67.3 36.2 %all-to-all-start = ((f32[8,1,82944]{2,1,0:T(1,128)}), f32[8,1,82944]{2,1,0:T(1,128)S(1)}, u32[]{:S(2)}, u32[]{:S(2)}) async-start(f32[8,1,82944]{2,1,0:T(1,128)} %reshape.223), calls=%async_computation | async-start | bytes 5308416 | tf_op jit(solution)/shard_map/all_to_all | solution.py:138
  72.6 112.7 %copy-start.5 = (f32[192,384]{1,0:T(8,128)}, f32[192,384]{1,0:T(8,128)S(1)}, u32[]{:S(2)}) copy-start(f32[192,384]{1,0:T(8,128)S(1)} %fusion.107) | copy-start | bytes 884740
  73.7 126.3 %copy-start.8 = (f32[192,384]{1,0:T(8,128)}, f32[192,384]{1,0:T(8,128)S(1)}, u32[]{:S(2)}) copy-start(f32[192,384]{1,0:T(8,128)S(1)} %fusion.106) | copy-start | bytes 884740
  179.4 20.7 %slice-start.2 = ((s8[7077888]{0:T(1024)(128)(4,1)}), s8[2883584]{0:T(1024)(128)(4,1)S(1)}, s32[]{:S(2)}) async-start(s8[7077888]{0:T(1024)(128)(4,1)} %bitcast.129), calls=%async_computation.10 | async-start | bytes 5767168
  179.4 120.6 %all-to-all-start.3 = ((f32[4,1,331776]{2,1,0:T(1,128)}), f32[4,1,331776]{2,1,0:T(1,128)}, u32[]{:S(2)}, u32[]{:S(2)}) async-start(f32[4,1,331776]{2,1,0:T(1,128)} %reshape.225), calls=%async_computation.3 | async-start | bytes 10616832 | tf_op jit(solution)/shard_map/all_to_all | solution.py:142
  185.3 14.7 %slice-start.3 = ((s8[7077888]{0:T(1024)(128)(4,1)}), s8[4194304]{0:T(1024)(128)(4,1)S(1)}, s32[]{:S(2)}) async-start(s8[7077888]{0:T(1024)(128)(4,1)} %bitcast.129), calls=%async_computation.11 | async-start | bytes 8388608
  300.0 121.6 %all-to-all-start.2 = ((f32[4,1,331776]{2,1,0:T(1,128)}), f32[4,1,331776]{2,1,0:T(1,128)}, u32[]{:S(2)}, u32[]{:S(2)}) async-start(f32[4,1,331776]{2,1,0:T(1,128)} %reshape.227), calls=%async_computation.2 | async-start | bytes 10616832 | tf_op jit(solution)/shard_map/all_to_all | solution.py:143
  517.0 15.8 %copy-start.4 = (f32[3,96,24,192]{3,2,1,0:T(8,128)S(1)}, f32[3,96,24,192]{3,2,1,0:T(8,128)}, u32[]{:S(2)}) copy-start(f32[3,96,24,192]{3,2,1,0:T(8,128)} %copy.105) | copy-start | bytes 15925252
  517.0 32.0 %slice-start.4 = ((s8[7077888]{0:T(1024)(128)(4,1)}), s8[4194304]{0:T(1024)(128)(4,1)S(1)}, s32[]{:S(2)}) async-start(s8[7077888]{0:T(1024)(128)(4,1)} %bitcast.134), calls=%async_computation.12 | async-start | bytes 8388608
  532.8 16.1 %slice-start.5 = ((s8[7077888]{0:T(1024)(128)(4,1)}), s8[2883584]{0:T(1024)(128)(4,1)S(1)}, s32[]{:S(2)}) async-start(s8[7077888]{0:T(1024)(128)(4,1)} %bitcast.134), calls=%async_computation.13 | async-start | bytes 5767168
  585.0 17.8 %copy-start = (f32[3,24,96,384]{3,1,2,0:T(8,128)}, f32[3,24,96,384]{3,1,2,0:T(8,128)S(1)}, u32[]{:S(2)}) copy-start(f32[3,24,96,384]{3,1,2,0:T(8,128)S(1)} %maximum_bitcast_fusion) | copy-start | bytes 31850500
  607.6 21.8 %copy-start.1 = (f32[3,24,96,384]{3,1,2,0:T(8,128)}, f32[3,24,96,384]{3,1,2,0:T(8,128)S(1)}, u32[]{:S(2)}) copy-start(f32[3,24,96,384]{3,1,2,0:T(8,128)S(1)} %fusion) | copy-start | bytes 31850500
  636.4 159.9 %all-to-all-start.4 = ((f32[3,192,24,96]{3,2,0,1:T(8,128)}), f32[3,192,24,96]{3,2,0,1:T(8,128)}, u32[]{:S(2)}, u32[]{:S(2)}) async-start(f32[3,192,24,96]{3,2,0,1:T(8,128)} %copy.116), calls=%async_computation.4 | async-start | bytes 14155776 | tf_op jit(solution)/shard_map/all_to_all | solution.py:154
  641.8 19.6 %copy-start.2 = (f32[3,24,96,384]{3,1,2,0:T(8,128)S(1)}, f32[3,24,96,384]{3,1,2,0:T(8,128)}, u32[]{:S(2)}) copy-start(f32[3,24,96,384]{3,1,2,0:T(8,128)} %copy-done.1) | copy-start | bytes 31850500
  796.4 160.3 %all-to-all-start.5 = ((f32[3,192,24,96]{3,2,0,1:T(8,128)}), f32[3,192,24,96]{3,2,0,1:T(8,128)}, u32[]{:S(2)}, u32[]{:S(2)}) async-start(f32[3,192,24,96]{3,2,0,1:T(8,128)} %copy.120), calls=%async_computation.5 | async-start | bytes 14155776 | tf_op jit(solution)/shard_map/all_to_all | solution.py:155
  1002.2 14.2 %slice-start.6 = ((s8[5308416]{0:T(1024)(128)(4,1)}), s8[1114112]{0:T(1024)(128)(4,1)S(1)}, s32[]{:S(2)}) async-start(s8[5308416]{0:T(1024)(128)(4,1)} %bitcast.140), calls=%async_computation.14 | async-start | bytes 2228224
  1002.2 39.2 %all-to-all-start.7 = ((f32[8,1,82944]{2,1,0:T(1,128)}), f32[8,1,82944]{2,1,0:T(1,128)}, u32[]{:S(2)}, u32[]{:S(2)}) async-start(f32[8,1,82944]{2,1,0:T(1,128)} %reshape.231), calls=%async_computation.7 | async-start | bytes 5308416 | tf_op jit(solution)/shard_map/all_to_all | solution.py:160
  1041.4 36.9 %all-to-all-start.6 = ((f32[8,1,82944]{2,1,0:T(1,128)}), f32[8,1,82944]{2,1,0:T(1,128)S(1)}, u32[]{:S(2)}, u32[]{:S(2)}) async-start(f32[8,1,82944]{2,1,0:T(1,128)} %reshape.229), calls=%async_computation.6 | async-start | bytes 5308416 | tf_op jit(solution)/shard_map/all_to_all | solution.py:159
  1124.8 14.8 %copy-start.9 = (f32[3,48,4608]{2,1,0:T(8,128)S(1)}, f32[3,48,4608]{2,1,0:T(8,128)}, u32[]{:S(2)}) copy-start(f32[3,48,4608]{2,1,0:T(8,128)} %param.1) | copy-start | bytes 7962628
  1124.9 7.2 collective-permute-start
  1126.3 7.2 collective-permute-start.1
  1134.5 31.0 %collective-permute-start.2 = (f32[3,52,2,192]{3,1,2,0:T(8,128)}, f32[3,52,2,192]{3,1,2,0:T(8,128)}, u32[]{:S(2)}, u32[]{:S(2)}) collective-permute-start(f32[3,52,2,192]{3,1,2,0:T(8,128)} %get-tuple-element.11), channel_id=1, source_target_pairs={{1,0},{2,1},{3,2},{4,3},{5,4},{6,5},{7,6},{9,8},{10,9},{11,10},{12... | collective-permute-start | bytes 718856 | tf_op jit(solution)/shard_map/ppermute | solution.py:23
  1135.8 29.7 %collective-permute-start.3 = (f32[3,52,2,192]{3,1,2,0:T(8,128)}, f32[3,52,2,192]{3,1,2,0:T(8,128)}, u32[]{:S(2)}, u32[]{:S(2)}) collective-permute-start(f32[3,52,2,192]{3,1,2,0:T(8,128)} %get-tuple-element.10), channel_id=1, source_target_pairs={{0,1},{1,2},{2,3},{3,4},{4,5},{5,6},{6,7},{8,9},{9,10},{10,11},{11... | collective-permute-start | bytes 718856 | tf_op jit(solution)/shard_map/ppermute | solution.py:22
  (11 other events, 60.6 us)
where the time goes:
time: 1200 us; the launch traced here: 1190 us
  local copies, waits for them, and re-layouts  348 us (29%)
  waiting for transfers between devices  318 us (26%)
  matrix products  266 us (22%)
  other arithmetic  202 us (17%)
  starting transfers between devices  53.3 us (4%)
    dot_general x20, matrix products, product(): return jnp.einsum(einsum_form, first, second, precision=highest)  266 us
    all_to_all x2, waiting for transfers between devices, on_device(): lax.all_to_all(pair[0], 'px', split_axis=1, concat_axis=3, tiled=True)  170 us
    unnamed x58, local copies, waits for them, and re-layouts  134 us
    all_to_all x2, waiting for transfers between devices, on_device(): lax.all_to_all(pair[1], 'px', split_axis=1, concat_axis=3, tiled=True)  127 us
    all_to_all x1, other arithmetic, on_device(): lax.all_to_all(pair[0], 'px', split_axis=1, concat_axis=3, tiled=True)  53.4 us
    all_to_all x1, other arithmetic, on_device(): lax.all_to_all(pair[1], 'px', split_axis=1, concat_axis=3, tiled=True)  53.2 us
    all_to_all x5, local copies, waits for them, and re-layouts, on_device(): lax.all_to_all(pair[0], 'px', split_axis=1, concat_axis=3, tiled=True)  46.7 us
    all_to_all x5, local copies, waits for them, and re-layouts, on_device(): lax.all_to_all(pair[1], 'px', split_axis=1, concat_axis=3, tiled=True)  46.6 us
  transfers between devices with their start and end apart: 12, of which 9 were waited for; matrix products, arithmetic and copies ran while one was open for 31% of the time, Pallas kernels for 0%

commit v1 on v0

--- a/solution.py
+++ b/solution.py
@@ -2,14 +2,467 @@
 
 import jax
 import jax.numpy as jnp
+import numpy as np
 from jax import lax
+from jax.experimental import pallas as pl
+from jax.experimental.pallas import tpu as pltpu
 from jax.sharding import PartitionSpec as P
-
-G = 192
-
 
 smoothing = 1.0
 highest = lax.Precision.HIGHEST
+f32 = jnp.float32
+bf16 = jnp.bfloat16
+CHUNKS = 2
+LANES = 128
+
+
+def split_table(table):
+    high = table.astype(np.float32).astype(jnp.bfloat16)
+    low = (table - high.astype(np.float64)).astype(np.float32).astype(jnp.bfloat16)
+    return high, low
+
+
+def waves(modes, length):
+    return np.asarray(modes, np.float64) * (2.0 * math.pi / length)
+
+
+def basis(points, modes, kinds, length):
+    angle = (np.arange(points)[:, None] * np.asarray(modes)[None, :] % length) * (
+        2.0 * math.pi / length
+    )
+    return np.where(np.asarray(kinds)[None, :] == 0, np.cos(angle), np.sin(angle))
+
+
+def weights(modes, length):
+    return np.where(np.asarray(modes) == 0, 1.0, 2.0) / length
+
+
+def lane_order(modes):
+    full = modes // LANES * LANES
+    index, kind = [], []
+    for start in range(0, full, LANES):
+        for k in (0, 1):
+            index += list(range(start, start + LANES))
+            kind += [k] * LANES
+    for k in (0, 1):
+        index += list(range(full, modes))
+        kind += [k] * (modes - full)
+    return np.array(index), np.array(kind)
+
+
+def dot(first, second, dims):
+    return lax.dot_general(first, second, (dims, ((), ())), preferred_element_type=f32)
+
+
+NN = ((1,), (0,))
+NT = ((1,), (1,))
+TN = ((0,), (0,))
+
+
+def halves(value):
+    high = value.astype(bf16)
+    low = (value - high.astype(f32)).astype(bf16)
+    return high, low
+
+
+def depth_forward(shard, table, sizes, chunk):
+    rows, cols, G, devices, kept, lanes = sizes
+    units = 6 * kept
+    block = 2 * kept * devices
+    tiles = lanes // LANES
+
+    def kernel(shard_ref, table_ref, out_ref, high_ref, low_ref, mid_ref):
+        table_high, table_low = table_ref[0], table_ref[1]
+        for c in range(3):
+            for y in range(cols):
+                high, low = halves(shard_ref[c, :, y * G : (y + 1) * G])
+                high_ref[y * rows : (y + 1) * rows, :] = high
+                low_ref[y * rows : (y + 1) * rows, :] = low
+            mid_ref[c * block : (c + 1) * block, :] = (
+                dot(table_high, high_ref[...], NT)
+                + dot(table_high, low_ref[...], NT)
+                + dot(table_low, high_ref[...], NT)
+            )
+        fill = [jnp.zeros((devices, lanes - units * rows), f32)] if lanes > units * rows else []
+        for y in range(cols):
+            pieces = [
+                mid_ref[u * devices : (u + 1) * devices, y * rows : (y + 1) * rows]
+                for u in range(units)
+            ]
+            line = jnp.concatenate(pieces + fill, axis=1)
+            for t in range(tiles):
+                at = pl.ds(t * cols + y, devices, stride=tiles * cols)
+                out_ref[at, :] = line[:, t * LANES : (t + 1) * LANES]
+
+    return pl.pallas_call(
+        kernel,
+        out_shape=jax.ShapeDtypeStruct((devices * tiles * cols, LANES), f32),
+        scratch_shapes=[
+            pltpu.VMEM((rows * cols, G), bf16),
+            pltpu.VMEM((rows * cols, G), bf16),
+            pltpu.VMEM((3 * block, rows * cols), f32),
+        ],
+        cost_estimate=pl.CostEstimate(
+            flops=18 * block * G * rows * cols,
+            bytes_accessed=4 * (3 * rows * cols * G + devices * cols * lanes),
+            transcendentals=0,
+        ),
+        name="depth_forward",
+    )(shard, table)
+
+
+def depth_inverse(lines, table, before, sizes):
+    rows, cols, G, devices, kept, lanes = sizes
+    units = 6 * kept
+    block = 2 * kept * devices
+    tiles = lanes // LANES
+    extra = [] if before is None else [before]
+
+    def kernel(lines_ref, table_ref, *refs):
+        before_ref = refs[0] if before is not None else None
+        out_ref, mid_ref, done_ref = refs[len(extra) :]
+        for y in range(cols):
+            line = jnp.concatenate(
+                [
+                    lines_ref[pl.ds(t * cols + y, devices, stride=tiles * cols), :]
+                    for t in range(tiles)
+                ],
+                axis=1,
+            )
+            for u in range(units):
+                mid_ref[u * devices : (u + 1) * devices, y * rows : (y + 1) * rows] = line[
+                    :, u * rows : (u + 1) * rows
+                ]
+        table_high, table_low = table_ref[0], table_ref[1]
+        for c in range(3):
+            high, low = halves(mid_ref[c * block : (c + 1) * block, :].T)
+            done_ref[...] = (
+                dot(high, table_high, NN) + dot(low, table_high, NN) + dot(high, table_low, NN)
+            )
+            for y in range(0, cols, 2):
+                pair = jnp.concatenate(
+                    [done_ref[y * rows : (y + 1) * rows, :], done_ref[(y + 1) * rows : (y + 2) * rows, :]],
+                    axis=1,
+                )
+                if before_ref is not None:
+                    pair = pair + before_ref[c, :, y * G : (y + 2) * G]
+                out_ref[c, :, y * G : (y + 2) * G] = pair
+
+    return pl.pallas_call(
+        kernel,
+        out_shape=jax.ShapeDtypeStruct((3, rows, cols * G), f32),
+        scratch_shapes=[
+            pltpu.VMEM((3 * block, rows * cols), f32),
+            pltpu.VMEM((rows * cols, G), f32),
+        ],
+        cost_estimate=pl.CostEstimate(
+            flops=18 * block * G * rows * cols,
+            bytes_accessed=4 * (6 * rows * cols * G + devices * cols * lanes),
+            transcendentals=0,
+        ),
+        name="depth_inverse",
+    )(lines, table, *extra)
+
+
+def planes(lines, place, tables, sizes, chunk, groups):
+    rows, cols, G, devices, kept, lanes = sizes
+    units = 6 * kept
+    length = 2 * G
+    step = 16
+    unit_wave = 2.0 * math.pi / length
+    full = G // LANES * LANES
+
+    def kernel(place_ref, lines_ref, line_ref, wide_ref, inv_wide_ref, inv_line_ref,
+               kx_ref, ky_ref, out_ref, left_ref, spec_ref, turned_ref, back_ref):
+        line_high, line_low = line_ref[0], line_ref[1]
+        for p in range(groups):
+            high, low = halves(
+                jnp.concatenate(
+                    [lines_ref[p, :, t].reshape(G, LANES).T for t in range(lanes // LANES)], axis=0
+                )
+            )
+            done = dot(high, line_high, NN) + dot(low, line_high, NN) + dot(high, line_low, NN)
+            for u in range(units):
+                c, j, k = u // (2 * kept), u // 2 % kept, u % 2
+                at = (2 * c + k) * length
+                high, low = halves(done[u * rows : (u + 1) * rows, :])
+                for third, part in ((0, high), (1, low), (2, high)):
+                    left_ref[j, third * G + p * rows : third * G + (p + 1) * rows, at : at + length] = part
+
+        def one_depth(j, _):
+            index = (chunk * kept + j) * devices + place_ref[0]
+            kz = index.astype(f32) * unit_wave
+
+            def widen(u, _):
+                at = pl.multiple_of(u * length, LANES)
+                spec_ref[:, pl.ds(at, length)] = dot(
+                    wide_ref[...], left_ref[j, :, pl.ds(at, length)], NN
+                )
+                return 0
+
+            lax.fori_loop(0, 6, widen, 0)
+
+            def turn(r, _):
+                top = pl.multiple_of(r * step, step)
+                kx = kx_ref[pl.ds(top, step), :]
+
+                def store(c, k, half, lane, value):
+                    high, low = halves(value)
+                    at = (2 * c + k) * length + lane
+                    for third, part in ((0, high), (1, low), (2, high)):
+                        turned_ref[pl.ds(third * length + half * G + top, step), at : at + LANES] = part
+
+                def green_of(lane):
+                    ky = ky_ref[0:1, lane : lane + LANES]
+                    square = kx * kx + ky * ky + kz * kz
+                    return jnp.exp(-0.5 * smoothing * smoothing * square) / (
+                        square + jnp.where(square == 0.0, 1.0, 0.0)
+                    )
+
+                def load(c, k, half, lane):
+                    at = (2 * c + k) * length + lane
+                    return spec_ref[pl.ds(half * G + top, step), at : at + LANES]
+
+                def curl(lane_of, count, dy_of, green):
+                    gx = green * kx
+                    gz = green * kz
+                    got = {
+                        (c, k, h, t): load(c, k, h, lane_of[t])
+                        for c in range(3) for k in (0, 1) for h in (0, 1) for t in range(count)
+                    }
+
+                    def dx(c, k, h, t):
+                        value = gx * got[c, k, 1 - h, t]
+                        return value if h == 0 else -value
+
+                    def dz(c, k, h, t):
+                        value = gz * got[c, 1 - k, h, t]
+                        return value if k == 0 else -value
+
+                    def dy(c, k, h, t):
+                        return dy_of(got, c, k, h, t)
+
+                    for k in (0, 1):
+                        for h in (0, 1):
+                            for t in range(count):
+                                store(0, k, h, lane_of[t], dy(2, k, h, t) - dz(1, k, h, t))
+                                store(1, k, h, lane_of[t], dz(0, k, h, t) - dx(2, k, h, t))
+                                store(2, k, h, lane_of[t], dx(1, k, h, t) - dy(0, k, h, t))
+
+                for tile in range(full // LANES):
+                    lane = 2 * tile * LANES
+                    green = green_of(lane)
+                    gy = green * ky_ref[0:1, lane : lane + LANES]
+
+                    def dy_pair(got, c, k, h, t, gy=gy):
+                        value = gy * got[c, k, h, 1 - t]
+                        return value if t == 0 else -value
+
+                    curl((lane, lane + LANES), 2, dy_pair, green)
+                if full < G:
+                    lane = 2 * full
+                    green = green_of(lane)
+                    gy = green * ky_ref[0:1, lane : lane + LANES]
+
+                    def dy_roll(got, c, k, h, t):
+                        return gy * pltpu.roll(got[c, k, h, t], LANES // 2, 1)
+
+                    curl((lane,), 1, dy_roll, green)
+                return 0
+
+            lax.fori_loop(0, G // step, turn, 0)
+
+            for c in range(3):
+                for k in (0, 1):
+                    at = (2 * c + k) * length
+                    done = dot(inv_wide_ref[...], turned_ref[:, at : at + length], NN)
+                    high, low = halves(done)
+                    u = c * 2 * kept + k
+                    for p in range(groups):
+                        target = pl.ds(pl.multiple_of((u + 2 * j) * rows, 16), rows)
+                        for third, part in ((0, high), (1, low), (2, high)):
+                            back_ref[p, target, third * length : (third + 1) * length] = part[
+                                p * rows : (p + 1) * rows, :
+                            ]
+            return 0
+
+        lax.fori_loop(0, kept, one_depth, 0)
+        if lanes > units * rows:
+            back_ref[:, units * rows :, :] = jnp.zeros(
+                (groups, lanes - units * rows, 3 * length), bf16
+            )
+        for p in range(groups):
+            for t in range(lanes // LANES):
+                done = dot(inv_line_ref[...], back_ref[p, t * LANES : (t + 1) * LANES, :], NT)
+                out_ref[p, :, t] = done.reshape(G // cols, cols, LANES)
+
+    vmem = pl.BlockSpec(memory_space=pltpu.VMEM)
+    flops = 6 * (2 * groups * lanes * G * length + 12 * kept * length * G * length)
+    return pl.pallas_call(
+        kernel,
+        out_shape=jax.ShapeDtypeStruct(lines.shape, f32),
+        in_specs=[pl.BlockSpec(memory_space=pltpu.SMEM)] + [vmem] * 7,
+        out_specs=vmem,
+        scratch_shapes=[
+            pltpu.VMEM((kept, 3 * G, 6 * length), bf16),
+            pltpu.VMEM((length, 6 * length), f32),
+            pltpu.VMEM((3 * length, 6 * length), bf16),
+            pltpu.VMEM((groups, lanes, 3 * length), bf16),
+        ],
+        cost_estimate=pl.CostEstimate(
+            flops=flops, bytes_accessed=8 * groups * G * lanes, transcendentals=kept * G * G
+        ),
+        compiler_params=pltpu.CompilerParams(vmem_limit_bytes=60 * 1024 * 1024),
+        name="planes",
+    )(place, lines, *tables)
+
+
+def with_halo_parts(flow, cols, G):
+    def shifted(piece, axis, up):
+        devices = lax.axis_size(axis)
+        pairs = [(i, i + 1) for i in range(devices - 1)]
+        if not up:
+            pairs = [(j, i) for i, j in pairs]
+        return lax.ppermute(piece, axis, pairs)
+
+    rows = flow.shape[1]
+    return (
+        shifted(lax.slice_in_dim(flow, rows - 2, rows, axis=1), "px", True),
+        shifted(lax.slice_in_dim(flow, 0, 2, axis=1), "px", False),
+        shifted(lax.slice_in_dim(flow, (cols - 2) * G, cols * G, axis=2), "py", True),
+        shifted(lax.slice_in_dim(flow, 0, 2 * G, axis=2), "py", False),
+    )
+
+
+def stretch(field, flow, halos, sizes):
+    rows, cols, G = sizes[:3]
+    width = 2 * G
+
+    def kernel(field_ref, flow_ref, up_ref, down_ref, left_ref, right_ref, out_ref, ext_ref, tall_ref):
+        for c in range(3):
+            ext_ref[c, :, 0:width] = left_ref[c]
+            ext_ref[c, :, width : width + cols * G] = flow_ref[c]
+            ext_ref[c, :, width + cols * G :] = right_ref[c]
+            tall_ref[c, 6:8, :] = up_ref[c]
+            tall_ref[c, 8 : 8 + rows, :] = flow_ref[c]
+            tall_ref[c, 8 + rows : 10 + rows, :] = down_ref[c]
+        depth = lax.broadcasted_iota(jnp.int32, (rows, width), 1) % G
+
+        def combine(p1, m1, p2, m2):
+            return (8.0 * (p1 - m1) - (p2 - m2)) * (1.0 / 12.0)
+
+        def block(b, _):
+            at = pl.multiple_of(b * width, LANES)
+            for c in range(3):
+                here = flow_ref[c, :, pl.ds(at, width)]
+
+                def depth_shift(s):
+                    moved = pltpu.roll(here, (-s) % width, 1)
+                    inside = (depth + s >= 0) & (depth + s < G)
+                    return jnp.where(inside, moved, 0.0)
+
+                total = field_ref[2, :, pl.ds(at, width)] * combine(
+                    depth_shift(1), depth_shift(-1), depth_shift(2), depth_shift(-2)
+                )
+                window = ext_ref[c, :, pl.ds(at, 3 * width)]
+                total += field_ref[1, :, pl.ds(at, width)] * combine(
+                    window[:, 3 * G : 5 * G], window[:, G : 3 * G], window[:, 4 * G :], window[:, : 2 * G]
+                )
+                total += field_ref[0, :, pl.ds(at, width)] * combine(
+                    tall_ref[c, 9 : 9 + rows, pl.ds(at, width)],
+                    tall_ref[c, 7 : 7 + rows, pl.ds(at, width)],
+                    tall_ref[c, 10 : 10 + rows, pl.ds(at, width)],
+                    tall_ref[c, 6 : 6 + rows, pl.ds(at, width)],
+                )
+                out_ref[c, :, pl.ds(at, width)] = total
+            return 0
+
+        lax.fori_loop(0, cols // 2, block, 0)
+
+    return pl.pallas_call(
+        kernel,
+        out_shape=jax.ShapeDtypeStruct(flow.shape, f32),
+        scratch_shapes=[
+            pltpu.VMEM((3, rows, cols * G + 2 * width), f32),
+            pltpu.VMEM((3, rows + 16, cols * G), f32),
+        ],
+        cost_estimate=pl.CostEstimate(
+            flops=60 * flow.size, bytes_accessed=12 * flow.size, transcendentals=0
+        ),
+        name="stretch",
+    )(field, flow, *halos)
+
+
+def fast_sizes(vorticity):
+    rows = vorticity.shape[1]
+    G = rows * lax.axis_size("px")
+    cols = vorticity.shape[2] // G
+    devices = lax.axis_size("px") * lax.axis_size("py")
+    if rows % 16 or cols % 8 or G % (CHUNKS * devices) or G % LANES not in (0, LANES // 2):
+        return None
+    kept = G // (CHUNKS * devices)
+    lanes = -(-6 * kept * rows // LANES) * LANES
+    return rows, cols, G, devices, kept, lanes
+
+
+def triple(table, axis):
+    high, low = split_table(table)
+    return np.concatenate([high, high, low], axis=axis)
+
+
+def fast(vorticity, sizes):
+    rows, cols, G, devices, kept, lanes = sizes
+    length = 2 * G
+    groups = lax.axis_size("px")
+    tiles = lanes // LANES
+    axes = ("px", "py")
+    place = lax.axis_index(axes).astype(jnp.int32).reshape(1)
+
+    lane_modes, lane_kinds = lane_order(G)
+    row_modes = np.concatenate([np.arange(G)] * 2)
+    row_kinds = np.repeat([0, 1], G)
+    line = np.stack(split_table(basis(G, lane_modes, lane_kinds, length)))
+    wide = triple(basis(G, row_modes, row_kinds, length).T, 1)
+    inv_wide = triple(basis(G, row_modes, row_kinds, length) * weights(row_modes, length), 1)
+    inv_line = triple(basis(G, lane_modes, lane_kinds, length) * weights(lane_modes, length), 1)
+    kx = np.broadcast_to(waves(np.arange(G), length)[:, None], (G, LANES)).astype(np.float32)
+    signs = np.where(lane_kinds == 0, 1.0, -1.0)
+    full = G // LANES * LANES
+    signs[: 2 * full] = 1.0
+    ky = np.broadcast_to((waves(lane_modes, length) * signs)[None, :], (8, length)).astype(np.float32)
+    tables = tuple(jnp.asarray(t) for t in (line, wide, inv_wide, inv_line, kx, ky))
+
+    def depth_tables(chunk):
+        modes = np.array([
+            (chunk * kept + j) * devices + d
+            for j in range(kept) for k in (0, 1) for d in range(devices)
+        ])
+        kinds = np.array([k for j in range(kept) for k in (0, 1) for d in range(devices)])
+        table = basis(G, modes, kinds, length)
+        forward = np.stack(split_table(table.T))
+        inverse = np.stack(split_table((table * weights(modes, length)).T))
+        return jnp.asarray(forward), jnp.asarray(inverse)
+
+    def exchange(value):
+        value = value.reshape(devices, tiles * cols, LANES)
+        return lax.all_to_all(value, axes, split_axis=0, concat_axis=0, tiled=True)
+
+    arrived = []
+    for chunk in range(CHUNKS):
+        sent = depth_forward(vorticity, depth_tables(chunk)[0], sizes, chunk)
+        arrived.append(exchange(sent))
+    returned = []
+    for chunk in range(CHUNKS):
+        lines = arrived[chunk].reshape(groups, G // cols, tiles, cols, LANES)
+        done = planes(lines, place, tables, sizes, chunk, groups)
+        returned.append(exchange(done))
+    flow = None
+    for chunk in range(CHUNKS):
+        flow = depth_inverse(
+            returned[chunk].reshape(devices * tiles * cols, LANES), depth_tables(chunk)[1], flow, sizes
+        )
+    halos = with_halo_parts(flow, cols, G)
+    return flow, stretch(vorticity, flow, halos, sizes)
 
 
 def with_halo(shard, sides, width):
@@ -117,8 +570,9 @@
     return (8.0 * near - far) / 12.0
 
 
-def on_device(vorticity):
+def general(vorticity):
     block_rows = vorticity.shape[1]
+    G = block_rows * lax.axis_size("px")
     block_cols = vorticity.shape[2] // G
     field = vorticity.reshape(3, block_rows, block_cols, G)
     length = 2 * G
@@ -176,6 +630,11 @@
     )
 
 
+def on_device(vorticity):
+    sizes = fast_sizes(vorticity)
+    return general(vorticity) if sizes is None else fast(vorticity, sizes)
+
+
 def solution(mesh):
     in_specs = (P(None, "px", "py"),)
     out_specs = (P(None, "px", "py"), P(None, "px", "py"))

time: 1200 us -> 321 us (0.27)
  local copies, waits for them, and re-layouts: 348 us -> 8.29 us
  matrix products: 266 us -> 0 us
  other arithmetic: 202 us -> 0 us
  waiting for transfers between devices: 318 us -> 186 us
  Pallas kernels: 0 us -> 95.1 us
  starting transfers between devices: 53.3 us -> 30.2 us
    dot_general x20 -> x0, matrix products: 266 us -> none  [product(): return jnp.einsum(einsum_form, first, second, precision=highest)]
    all_to_all x6 -> x0, other arithmetic: 146 us -> none  [the longest x1 53.4 us: on_device(): lax.all_to_all(pair[0], 'px', split_axis=1, concat_axis=3, tiled=True)]
    all_to_all x8 -> x4, waiting for transfers between devices: 316 us -> 183 us  [exchange(): return lax.all_to_all(value, axes, split_axis=0, concat_axis=0, tiled=True)]
    unnamed x58 -> x14, local copies, waits for them, and re-layouts: 134 us -> 5.99 us
    all_to_all x15 -> x0, local copies, waits for them, and re-layouts: 116 us -> none  [the longest x5 46.7 us: on_device(): lax.all_to_all(pair[0], 'px', split_axis=1, concat_axis=3, tiled=True)]
    pallas_call x0 -> x7, Pallas kernels: none -> 95.1 us  [the longest x2 54.1 us: planes(): pl.pallas_call(kernel, out_shape=jax.ShapeDtypeStruct(lines.shape, f32),...]
    add x4 -> x0, local copies, waits for them, and re-layouts: 29.2 us -> none  [the longest x2 14.2 us: backward_left(): product(einsum_form, cosine_table, imag_part)]
    sub x4 -> x0, local copies, waits for them, and re-layouts: 29 us -> none  [the longest x2 14.3 us: backward_left(): product(einsum_form, cosine_table, real_part)]
  transfers between devices with their start and end apart: 12 -> 8, of which waited for: 9 -> 6; matrix products, arithmetic and copies ran while one was open for 31% -> 0% of each run, Pallas kernels for 0% -> 21%
where the time goes in v1:
time: 321 us; the launch traced here: 320 us
  waiting for transfers between devices  186 us (58%)
  Pallas kernels  95.1 us (30%)
  starting transfers between devices  30.2 us (9%)
  local copies, waits for them, and re-layouts  8.29 us (3%)
    all_to_all x4, waiting for transfers between devices, exchange(): return lax.all_to_all(value, axes, split_axis=0, concat_axis=0, tiled=True)  183 us
    pallas_call x2, Pallas kernels, planes(): pl.pallas_call(kernel, out_shape=jax.ShapeDtypeStruct(lines.shape, f32),...  54.1 us
    all_to_all x4, starting transfers between devices, exchange(): return lax.all_to_all(value, axes, split_axis=0, concat_axis=0, tiled=True)  20 us
    pallas_call x2, Pallas kernels, depth_inverse(): pl.pallas_call(kernel, out_shape=jax.ShapeDtypeStruct((3, rows, cols * G)...  15.6 us
    pallas_call x2, Pallas kernels, depth_forward(): pl.pallas_call(kernel, out_shape=jax.ShapeDtypeStruct((devices * tiles *...  13.9 us
    pallas_call x1, Pallas kernels, stretch(): pl.pallas_call(kernel, out_shape=jax.ShapeDtypeStruct(flow.shape, f32), s...  11.5 us
    ppermute x4, starting transfers between devices, shifted(): return lax.ppermute(piece, axis, pairs)  10.2 us
  transfers between devices with their start and end apart: 8, of which 6 were waited for; matrix products, arithmetic and copies ran while one was open for 0% of the time, Pallas kernels for 21%

profile of v1, /device:TPU:0, one launch (start us, length us, event | category | flops | bytes accessed | tf_op | source)
XLA Modules:
  0.0 320.2 jit_solution(2580056371281548971)
XLA Ops:
  0.6 7.0 %depth_forward.3 = f32[5376,128]{1,0:T(8,128)} custom-call(f32[3,48,4608]{2,1,0:T(8,128)} %field_ref.1, bf16[2,192,192]{2,1,0:T(8,128)(2,1)} %constant.36.clone.table_ref), custom_call_target="tpu_custom_call" | custom-call | flops 764411904 | bytes 5406720 | tf_op jit(solution)/shard_map/depth_forward/pallas_call | solution.py:97
  7.6 7.3 %all-to-all-start.2 = ((f32[32,168,128]{2,1,0:T(8,128)}), f32[32,168,128]{2,1,0:T(8,128)S(1)}, u32[]{:S(2)}, u32[]{:S(2)}) async-start(f32[32,168,128]{2,1,0:T(8,128)} %bitcast.11), calls=%async_computation.2 | async-start | bytes 5505024 | tf_op jit(solution)/shard_map/all_to_all | solution.py:448
  14.9 6.9 %depth_forward.2 = f32[5376,128]{1,0:T(8,128)} custom-call(f32[3,48,4608]{2,1,0:T(8,128)} %field_ref.1, bf16[2,192,192]{2,1,0:T(8,128)(2,1)} %constant.37.clone.table_ref), custom_call_target="tpu_custom_call" | custom-call | flops 764411904 | bytes 5406720 | tf_op jit(solution)/shard_map/depth_forward/pallas_call | solution.py:97
  21.8 56.0 %all-to-all-done.2 = f32[32,168,128]{2,1,0:T(8,128)S(1)} async-done(((f32[32,168,128]{2,1,0:T(8,128)}), f32[32,168,128]{2,1,0:T(8,128)S(1)}, u32[]{:S(2)}, u32[]{:S(2)}) %all-to-all-start.2) | async-done | bytes 2752544 | tf_op jit(solution)/shard_map/all_to_all | solution.py:448
  77.8 1.5 copy-done.2
  79.3 4.2 %all-to-all-start = ((f32[32,168,128]{2,1,0:T(8,128)}), f32[32,168,128]{2,1,0:T(8,128)S(1)}, u32[]{:S(2)}, u32[]{:S(2)}) async-start(f32[32,168,128]{2,1,0:T(8,128)} %bitcast.9), calls=%async_computation | async-start | bytes 5505024 | tf_op jit(solution)/shard_map/all_to_all | solution.py:448
  83.6 27.1 %planes.3 = f32[4,8,7,24,128]{4,3,2,1,0:T(8,128)} custom-call(s32[1]{0:T(128)} %bitcast.place_ref, f32[4,8,7,24,128]{4,3,2,1,0:T(8,128)} %bitcast.13, bf16[2,192,384]{2,1,0:T(8,128)(2,1)} %constant.30.clone.line_ref, bf16[384,576]{1,0:T(8,128)(2,1)} %constant.31.clone.wide_ref, bf16[192,1152]{1,0:T(8,128)(2,1)} %constant.32.clone.inv_wide_ref, ...), custom_call_target="tpu_custom_call" | custom-call | flops 9286189056 | bytes 5505024 | tf_op jit(solution)/shard_map/planes/pallas_call | solution.py:301
  110.6 35.8 %all-to-all-done = f32[32,168,128]{2,1,0:T(8,128)S(1)} async-done(((f32[32,168,128]{2,1,0:T(8,128)}), f32[32,168,128]{2,1,0:T(8,128)S(1)}, u32[]{:S(2)}, u32[]{:S(2)}) %all-to-all-start) | async-done | bytes 2752544 | tf_op jit(solution)/shard_map/all_to_all | solution.py:448
  146.4 1.5 copy-done.1
  147.9 4.1 %all-to-all-start.3 = ((f32[32,168,128]{2,1,0:T(8,128)}), f32[32,168,128]{2,1,0:T(8,128)S(1)}, u32[]{:S(2)}, u32[]{:S(2)}) async-start(f32[32,168,128]{2,1,0:T(8,128)} %bitcast.15), calls=%async_computation.3 | async-start | bytes 5505024 | tf_op jit(solution)/shard_map/all_to_all | solution.py:448
  152.1 27.0 %planes.2 = f32[4,8,7,24,128]{4,3,2,1,0:T(8,128)} custom-call(s32[1]{0:T(128)} %bitcast.place_ref, f32[4,8,7,24,128]{4,3,2,1,0:T(8,128)} %bitcast.12, bf16[2,192,384]{2,1,0:T(8,128)(2,1)} %constant.30.clone.line_ref, bf16[384,576]{1,0:T(8,128)(2,1)} %constant.31.clone.wide_ref, bf16[192,1152]{1,0:T(8,128)(2,1)} %constant.32.clone.inv_wide_ref, ...), custom_call_target="tpu_custom_call" | custom-call | flops 9286189056 | bytes 5505024 | tf_op jit(solution)/shard_map/planes/pallas_call | solution.py:301
  179.1 35.8 %all-to-all-done.3 = f32[32,168,128]{2,1,0:T(8,128)S(1)} async-done(((f32[32,168,128]{2,1,0:T(8,128)}), f32[32,168,128]{2,1,0:T(8,128)S(1)}, u32[]{:S(2)}, u32[]{:S(2)}) %all-to-all-start.3) | async-done | bytes 2752544 | tf_op jit(solution)/shard_map/all_to_all | solution.py:448
  214.9 1.5 copy-done
  216.4 4.3 %all-to-all-start.1 = ((f32[32,168,128]{2,1,0:T(8,128)}), f32[32,168,128]{2,1,0:T(8,128)}, u32[]{:S(2)}, u32[]{:S(2)}) async-start(f32[32,168,128]{2,1,0:T(8,128)} %bitcast.14), calls=%async_computation.1 | async-start | bytes 5505024 | tf_op jit(solution)/shard_map/all_to_all | solution.py:448
  220.7 7.3 %depth_inverse.2.refs_0_ = f32[3,48,4608]{2,1,0:T(8,128)} custom-call(f32[5376,128]{1,0:T(8,128)} %bitcast.10, bf16[2,192,192]{2,1,0:T(8,128)(2,1)} %constant.38.clone.table_ref), custom_call_target="tpu_custom_call" | custom-call | flops 764411904 | bytes 8060928 | tf_op jit(solution)/shard_map/depth_inverse/pallas_call | solution.py:151
  228.0 55.4 %all-to-all-done.1 = f32[32,168,128]{2,1,0:T(8,128)} async-done(((f32[32,168,128]{2,1,0:T(8,128)}), f32[32,168,128]{2,1,0:T(8,128)}, u32[]{:S(2)}, u32[]{:S(2)}) %all-to-all-start.1) | async-done | bytes 2752544 | tf_op jit(solution)/shard_map/all_to_all | solution.py:448
  283.5 8.3 %depth_inverse.3.flow_ref = f32[3,48,4608]{2,1,0:T(8,128)} custom-call(f32[5376,128]{1,0:T(8,128)} %bitcast.4.lines_ref, bf16[2,192,192]{2,1,0:T(8,128)(2,1)} %constant.39.clone.table_ref, f32[3,48,4608]{2,1,0:T(8,128)} %depth_inverse.2.refs_0_), custom_call_target="tpu_custom_call" | custom-call | flops 764411904 | bytes 8060928 | tf_op jit(solution)/shard_map/depth_inverse/pallas_call | solution.py:151
  292.8 1.3 collective-permute-start.3
  294.1 3.0 collective-permute-start.2
  297.2 1.2 fusion.1
  298.4 1.3 collective-permute-start.1
  299.7 4.6 %collective-permute-start = (f32[3,2,4608]{2,1,0:T(2,128)S(1)}, f32[3,2,4608]{2,1,0:T(2,128)S(1)}, u32[]{:S(2)}, u32[]{:S(2)}) collective-permute-start(f32[3,2,4608]{2,1,0:T(2,128)S(1)} %get-tuple-element.5), channel_id=1, source_target_pairs={{0,8},{8,16},{16,24},{1,9},{9,17},{17,25},{2,10},{10,18},{18,26},{... | collective-permute-start | bytes 331784 | tf_op jit(solution)/shard_map/ppermute | solution.py:326
  304.3 1.8 collective-permute-done.1.down_ref
  308.6 11.5 %stretch.1 = f32[3,48,4608]{2,1,0:T(8,128)} custom-call(f32[3,48,4608]{2,1,0:T(8,128)} %field_ref.1, f32[3,48,4608]{2,1,0:T(8,128)} %depth_inverse.3.flow_ref, f32[3,2,4608]{2,1,0:T(2,128)} %copy-done.6, f32[3,2,4608]{2,1,0:T(2,128)} %copy-done.5, f32[3,48,384]{2,1,0:T(8,128)} %copy-done.4, f32[3,48,384]{2,1,0:T(8,128)} %copy-done.3), custom_call_target="tpu_custom_call" | custom-call | flops 39813120 | bytes 7962624 | tf_op jit(solution)/shard_map/stretch/pallas_call | solution.py:382
  (15 shorter events, 3.7 us)
Async XLA Ops:
  7.6 70.2 %all-to-all-start.2 = ((f32[32,168,128]{2,1,0:T(8,128)}), f32[32,168,128]{2,1,0:T(8,128)S(1)}, u32[]{:S(2)}, u32[]{:S(2)}) async-start(f32[32,168,128]{2,1,0:T(8,128)} %bitcast.11), calls=%async_computation.2 | async-start | bytes 5505024 | tf_op jit(solution)/shard_map/all_to_all | solution.py:448
  77.8 1.5 copy-start.2
  79.3 67.1 %all-to-all-start = ((f32[32,168,128]{2,1,0:T(8,128)}), f32[32,168,128]{2,1,0:T(8,128)S(1)}, u32[]{:S(2)}, u32[]{:S(2)}) async-start(f32[32,168,128]{2,1,0:T(8,128)} %bitcast.9), calls=%async_computation | async-start | bytes 5505024 | tf_op jit(solution)/shard_map/all_to_all | solution.py:448
  146.4 1.5 copy-start.1
  147.9 67.0 %all-to-all-start.3 = ((f32[32,168,128]{2,1,0:T(8,128)}), f32[32,168,128]{2,1,0:T(8,128)S(1)}, u32[]{:S(2)}, u32[]{:S(2)}) async-start(f32[32,168,128]{2,1,0:T(8,128)} %bitcast.15), calls=%async_computation.3 | async-start | bytes 5505024 | tf_op jit(solution)/shard_map/all_to_all | solution.py:448
  214.9 1.5 copy-start
  216.4 67.1 %all-to-all-start.1 = ((f32[32,168,128]{2,1,0:T(8,128)}), f32[32,168,128]{2,1,0:T(8,128)}, u32[]{:S(2)}, u32[]{:S(2)}) async-start(f32[32,168,128]{2,1,0:T(8,128)} %bitcast.14), calls=%async_computation.1 | async-start | bytes 5505024 | tf_op jit(solution)/shard_map/all_to_all | solution.py:448
  292.8 14.4 %collective-permute-start.3 = (f32[3,48,384]{2,1,0:T(8,128)S(1)}, f32[3,48,384]{2,1,0:T(8,128)S(1)}, u32[]{:S(2)}, u32[]{:S(2)}) collective-permute-start(f32[3,48,384]{2,1,0:T(8,128)S(1)} %get-tuple-element.2), channel_id=1, source_target_pairs={{1,0},{2,1},{3,2},{4,3},{5,4},{6,5},{7,6},{9,8},{10,9},{11,10},{12... | collective-permute-start | bytes 663560 | tf_op jit(solution)/shard_map/ppermute | solution.py:326
  294.1 13.1 %collective-permute-start.2 = (f32[3,48,384]{2,1,0:T(8,128)S(1)}, f32[3,48,384]{2,1,0:T(8,128)S(1)}, u32[]{:S(2)}, u32[]{:S(2)}) collective-permute-start(f32[3,48,384]{2,1,0:T(8,128)S(1)} %get-tuple-element.3), channel_id=1, source_target_pairs={{0,1},{1,2},{2,3},{3,4},{4,5},{5,6},{6,7},{8,9},{9,10},{10,11},{11... | collective-permute-start | bytes 663560 | tf_op jit(solution)/shard_map/ppermute | solution.py:326
  298.4 7.6 %collective-permute-start.1 = (f32[3,2,4608]{2,1,0:T(2,128)S(1)}, f32[3,2,4608]{2,1,0:T(2,128)S(1)}, u32[]{:S(2)}, u32[]{:S(2)}) collective-permute-start(f32[3,2,4608]{2,1,0:T(2,128)S(1)} %get-tuple-element.4), channel_id=1, source_target_pairs={{8,0},{16,8},{24,16},{9,1},{17,9},{25,17},{10,2},{18,10},{26,18},{... | collective-permute-start | bytes 331784 | tf_op jit(solution)/shard_map/ppermute | solution.py:326
  299.7 7.5 %collective-permute-start = (f32[3,2,4608]{2,1,0:T(2,128)S(1)}, f32[3,2,4608]{2,1,0:T(2,128)S(1)}, u32[]{:S(2)}, u32[]{:S(2)}) collective-permute-start(f32[3,2,4608]{2,1,0:T(2,128)S(1)} %get-tuple-element.5), channel_id=1, source_target_pairs={{0,8},{8,16},{16,24},{1,9},{9,17},{17,25},{2,10},{10,18},{18,26},{... | collective-permute-start | bytes 331784 | tf_op jit(solution)/shard_map/ppermute | solution.py:326
  306.0 1.2 copy-start.5
  307.2 0.6 copy-start.6
  307.2 0.7 copy-start.3
  308.0 0.7 copy-start.4

commit v2 on v1

v2 whole, which is shorter than its diff:
```python
import math

import jax
import jax.numpy as jnp
import numpy as np
from jax import lax
from jax.experimental import pallas as pl
from jax.experimental.pallas import tpu as pltpu
from jax.sharding import PartitionSpec as P

smoothing = 1.0
highest = lax.Precision.HIGHEST
f32 = jnp.float32
bf16 = jnp.bfloat16
LANES = 128
SUB = 8
PLANES_VMEM = 44 * 1024 * 1024


def split_table(table):
    high = table.astype(np.float32).astype(jnp.bfloat16)
    low = (table - high.astype(np.float64)).astype(np.float32).astype(jnp.bfloat16)
    return high, low


def waves(modes, length):
    return np.asarray(modes, np.float64) * (2.0 * math.pi / length)


def basis(points, modes, kinds, length):
    angle = (np.arange(points)[:, None] * np.asarray(modes)[None, :] % length) * (
        2.0 * math.pi / length
    )
    return np.where(np.asarray(kinds)[None, :] == 0, np.cos(angle), np.sin(angle))


def weights(modes, length):
    return np.where(np.asarray(modes) == 0, 1.0, 2.0) / length


def lane_order(modes):
    full = modes // LANES * LANES
    index, kind = [], []
    for start in range(0, full, LANES):
        for k in (0, 1):
            index += list(range(start, start + LANES))
            kind += [k] * LANES
    for k in (0, 1):
        index += list(range(full, modes))
        kind += [k] * (modes - full)
    return np.array(index), np.array(kind)


def dot(first, second, dims):
    return lax.dot_general(first, second, (dims, ((), ())), preferred_element_type=f32)


NN = ((1,), (0,))
NT = ((1,), (1,))
TN = ((0,), (0,))


def halves(value):
    high = value.astype(bf16)
    low = (value - high.astype(f32)).astype(bf16)
    return high, low


class Sizes:
    def __init__(self, rows, cols, G, devices, groups):
        self.rows, self.cols, self.G = rows, cols, G
        self.devices, self.groups = devices, groups
        self.bands = cols // SUB
        self.length = 2 * G
        total = G // devices
        first = max(1, total * 2 // 3)
        self.chunks = [(0, first), (first, total - first)] if total > first else [(0, first)]

    def units(self, kept):
        return 6 * kept

    def tiles(self, kept):
        return -(-self.bands * self.units(kept) * self.rows // LANES)


def fast_sizes(vorticity):
    rows = vorticity.shape[1]
    groups = lax.axis_size("px")
    G = rows * groups
    cols = vorticity.shape[2] // G
    devices = groups * lax.axis_size("py")
    if rows % 16 or cols % (2 * SUB) not in (0, SUB) or cols % SUB or cols % 2:
        return None
    if G % devices or devices % SUB or G % LANES not in (0, LANES // 2):
        return None
    return Sizes(rows, cols, G, devices, groups)


def depth_forward(shard, table, size, kept):
    rows, cols, G, devices = size.rows, size.cols, size.G, size.devices
    units, tiles, bands = size.units(kept), size.tiles(kept), size.bands
    block = 2 * kept * devices
    used = bands * units * rows

    def kernel(shard_ref, table_ref, out_ref, high_ref, low_ref, mid_ref):
        def component(c, _):
            for y in range(cols):
                high, low = halves(shard_ref[c, :, y * G : (y + 1) * G])
                high_ref[y * rows : (y + 1) * rows, :] = high
                low_ref[y * rows : (y + 1) * rows, :] = low
            mid_ref[pl.ds(pl.multiple_of(c * block, SUB), block), :] = (
                dot(table_ref[0], high_ref[...], NT)
                + dot(table_ref[0], low_ref[...], NT)
                + dot(table_ref[1], high_ref[...], NT)
            )
            return 0

        lax.fori_loop(0, 3, component, 0)
        fill = [jnp.zeros((devices, tiles * LANES - used), f32)] if tiles * LANES > used else []
        for s in range(SUB):
            pieces = [
                mid_ref[
                    u * devices : (u + 1) * devices,
                    (SUB * band + s) * rows : (SUB * band + s + 1) * rows,
                ]
                for band in range(bands)
                for u in range(units)
            ]
            line = jnp.concatenate(pieces + fill, axis=1)
            for t in range(tiles):
                at = pl.ds(t * SUB + s, devices, stride=tiles * SUB)
                out_ref[at, :] = line[:, t * LANES : (t + 1) * LANES]

    return pl.pallas_call(
        kernel,
        out_shape=jax.ShapeDtypeStruct((devices * tiles * SUB, LANES), f32),
        scratch_shapes=[
            pltpu.VMEM((rows * cols, G), bf16),
            pltpu.VMEM((rows * cols, G), bf16),
            pltpu.VMEM((3 * block, rows * cols), f32),
        ],
        cost_estimate=pl.CostEstimate(
            flops=18 * block * G * rows * cols,
            bytes_accessed=4 * (3 * rows * cols * G + devices * tiles * SUB * LANES),
            transcendentals=0,
        ),
        name="depth_forward",
    )(shard, table)


def depth_inverse(lines, table, before, size, kept, slabs):
    rows, cols, G, devices = size.rows, size.cols, size.G, size.devices
    units, tiles, bands = size.units(kept), size.tiles(kept), size.bands
    block = 2 * kept * devices
    extra = [] if before is None else [before]
    outs = [jax.ShapeDtypeStruct((3, rows, cols * G), f32)]
    if slabs:
        outs += [jax.ShapeDtypeStruct((3, 2, cols * G), f32)] * 2
        outs += [jax.ShapeDtypeStruct((3, rows, 2 * G), f32)] * 2

    def kernel(lines_ref, table_ref, *refs):
        before_ref = refs[0] if before is not None else None
        out_ref, *slab_refs = refs[len(extra) : len(extra) + len(outs)]
        mid_ref, done_ref = refs[len(extra) + len(outs) :]
        for s in range(SUB):
            line = jnp.concatenate(
                [
                    lines_ref[pl.ds(t * SUB + s, devices, stride=tiles * SUB), :]
                    for t in range(tiles)
                ],
                axis=1,
            )
            for band in range(bands):
                y = SUB * band + s
                for u in range(units):
                    at = (band * units + u) * rows
                    mid_ref[u * devices : (u + 1) * devices, y * rows : (y + 1) * rows] = line[
                        :, at : at + rows
                    ]

        def component(c, _):
            high, low = halves(mid_ref[pl.ds(pl.multiple_of(c * block, SUB), block), :].T)
            done_ref[...] = (
                dot(high, table_ref[0], NN)
                + dot(low, table_ref[0], NN)
                + dot(high, table_ref[1], NN)
            )
            for y in range(0, cols, 2):
                pair = jnp.concatenate(
                    [
                        done_ref[y * rows : (y + 1) * rows, :],
                        done_ref[(y + 1) * rows : (y + 2) * rows, :],
                    ],
                    axis=1,
                )
                if before_ref is not None:
                    pair = pair + before_ref[c, :, y * G : (y + 2) * G]
                out_ref[c, :, y * G : (y + 2) * G] = pair
                if slabs:
                    slab_refs[0][c, :, y * G : (y + 2) * G] = pair[rows - 2 :, :]
                    slab_refs[1][c, :, y * G : (y + 2) * G] = pair[:2, :]
                if slabs and y == cols - 2:
                    slab_refs[2][c] = pair
                if slabs and y == 0:
                    slab_refs[3][c] = pair
            return 0

        lax.fori_loop(0, 3, component, 0)

    return pl.pallas_call(
        kernel,
        out_shape=outs,
        scratch_shapes=[
            pltpu.VMEM((3 * block, rows * cols), f32),
            pltpu.VMEM((rows * cols, G), f32),
        ],
        cost_estimate=pl.CostEstimate(
            flops=18 * block * G * rows * cols,
            bytes_accessed=4 * (6 * rows * cols * G + devices * tiles * SUB * LANES),
            transcendentals=0,
        ),
        name="depth_inverse",
    )(lines, table, *extra)


def planes(lines, place, tables, size, kept):
    rows, cols, G, devices, groups = size.rows, size.cols, size.G, size.devices, size.groups
    units, tiles, bands, length = size.units(kept), size.tiles(kept), size.bands, size.length
    width = units * rows
    step = 16
    unit_wave = 2.0 * math.pi / length
    full = G // LANES * LANES
    others = G // cols

    def kernel(place_ref, lines_ref, line_ref, wide_ref, inv_wide_ref, inv_line_ref,
               kx_ref, ky_ref, out_ref, left_ref, spec_ref, turned_ref, back_ref):
        def arrive(p, _):
            flat = jnp.concatenate(
                [lines_ref[p, :, t].reshape(others * SUB, LANES).T for t in range(tiles)], axis=0
            )
            side = jnp.concatenate(
                [flat[band * width : (band + 1) * width, :] for band in range(bands)], axis=1
            )
            high, low = halves(side)
            done = (
                dot(high, line_ref[0], NN) + dot(low, line_ref[0], NN) + dot(high, line_ref[1], NN)
            )
            for u in range(units):
                c, j, k = u // (2 * kept), u // 2 % kept, u % 2
                at = (2 * c + k) * length
                high, low = halves(done[u * rows : (u + 1) * rows, :])
                for part, value in ((0, high), (1, low)):
                    target = pl.ds(pl.multiple_of(part * G + p * rows, 16), rows)
                    left_ref[j, target, at : at + length] = value
            return 0

        lax.fori_loop(0, groups, arrive, 0)

        def one_depth(j, _):
            index = (place_ref[1] + j) * devices + place_ref[0]
            kz = index.astype(f32) * unit_wave

            def widen(u, _):
                at = pl.ds(pl.multiple_of(u * length, LANES), length)
                spec_ref[:, at] = dot(wide_ref[:, :length], left_ref[j, :, at], NN) + dot(
                    wide_ref[:, length:], left_ref[j, :G, at], NN
                )
                return 0

            lax.fori_loop(0, 6, widen, 0)

            def turn(r, _):
                top = pl.multiple_of(r * step, step)
                kx = kx_ref[pl.ds(top, step), :]

                def store(c, k, half, lane, value):
                    at = (2 * c + k) * length + lane
                    for part, piece in zip((0, 1), halves(value)):
                        target = pl.ds(pl.multiple_of(part * length + half * G + top, step), step)
                        turned_ref[target, at : at + LANES] = piece

                def green_of(lane):
                    ky = ky_ref[0:1, lane : lane + LANES]
                    square = kx * kx + ky * ky + kz * kz
                    return jnp.exp(-0.5 * smoothing * smoothing * square) / (
                        square + jnp.where(square == 0.0, 1.0, 0.0)
                    )

                def load(c, k, half, lane):
                    at = (2 * c + k) * length + lane
                    target = pl.ds(pl.multiple_of(half * G + top, step), step)
                    return spec_ref[target, at : at + LANES]

                def curl(lane_of, dy_of, green):
                    gx = green * kx
                    gz = green * kz
                    many = range(len(lane_of))
                    got = {
                        (c, k, h, t): load(c, k, h, lane_of[t])
                        for c in range(3) for k in (0, 1) for h in (0, 1) for t in many
                    }

                    def dx(c, k, h, t):
                        value = gx * got[c, k, 1 - h, t]
                        return value if h == 0 else -value

                    def dz(c, k, h, t):
                        value = gz * got[c, 1 - k, h, t]
                        return value if k == 0 else -value

                    def dy(c, k, h, t):
                        return dy_of(got, c, k, h, t)

                    for k in (0, 1):
                        for h in (0, 1):
                            for t in many:
                                store(0, k, h, lane_of[t], dy(2, k, h, t) - dz(1, k, h, t))
                                store(1, k, h, lane_of[t], dz(0, k, h, t) - dx(2, k, h, t))
                                store(2, k, h, lane_of[t], dx(1, k, h, t) - dy(0, k, h, t))

                for tile in range(full // LANES):
                    lane = 2 * tile * LANES
                    green = green_of(lane)
                    gy = green * ky_ref[0:1, lane : lane + LANES]

                    def dy_pair(got, c, k, h, t, gy=gy):
                        value = gy * got[c, k, h, 1 - t]
                        return value if t == 0 else -value

                    curl((lane, lane + LANES), dy_pair, green)
                if full < G:
                    lane = 2 * full
                    green = green_of(lane)
                    gy = green * ky_ref[0:1, lane : lane + LANES]

                    def dy_roll(got, c, k, h, t):
                        return gy * pltpu.roll(got[c, k, h, t], LANES // 2, 1)

                    curl((lane,), dy_roll, green)
                return 0

            lax.fori_loop(0, G // step, turn, 0)

            def narrow(u, _):
                at = pl.ds(pl.multiple_of(u * length, LANES), length)
                done = dot(inv_wide_ref[:, : 2 * length], turned_ref[:, at], NN) + dot(
                    inv_wide_ref[:, 2 * length :], turned_ref[:length, at], NN
                )
                high, low = halves(done)
                unit = (u // 2) * (2 * kept) + 2 * j + u % 2
                target = pl.ds(pl.multiple_of(unit * rows, 16), rows)
                for p in range(groups):
                    for part, value in ((0, high), (1, low)):
                        back_ref[p, target, part * length : (part + 1) * length] = value[
                            p * rows : (p + 1) * rows, :
                        ]
                return 0

            lax.fori_loop(0, 6, narrow, 0)
            return 0

        lax.fori_loop(0, kept, one_depth, 0)

        def leave(p, _):
            done = dot(inv_line_ref[:, : 2 * length], back_ref[p], NT) + dot(
                inv_line_ref[:, 2 * length :], back_ref[p, :, :length], NT
            )
            pieces = [
                done[band * others * SUB : (band + 1) * others * SUB, :] for band in range(bands)
            ]
            if tiles * LANES > bands * width:
                pieces += [jnp.zeros((others * SUB, tiles * LANES - bands * width), f32)]
            line = jnp.concatenate(pieces, axis=1)
            for t in range(tiles):
                out_ref[p, :, t] = line[:, t * LANES : (t + 1) * LANES].reshape(others, SUB, LANES)
            return 0

        lax.fori_loop(0, groups, leave, 0)

    vmem = pl.BlockSpec(memory_space=pltpu.VMEM)
    flops = 6 * (4 * groups * width * G * length + 24 * kept * length * G * length)
    return pl.pallas_call(
        kernel,
        out_shape=jax.ShapeDtypeStruct(lines.shape, f32),
        in_specs=[pl.BlockSpec(memory_space=pltpu.SMEM)] + [vmem] * 7,
        out_specs=vmem,
        scratch_shapes=[
            pltpu.VMEM((kept, 2 * G, 6 * length), bf16),
            pltpu.VMEM((length, 6 * length), f32),
            pltpu.VMEM((2 * length, 6 * length), bf16),
            pltpu.VMEM((groups, width, 2 * length), bf16),
        ],
        cost_estimate=pl.CostEstimate(
            flops=flops, bytes_accessed=8 * lines.size, transcendentals=kept * G * G
        ),
        compiler_params=pltpu.CompilerParams(vmem_limit_bytes=PLANES_VMEM),
        name="planes",
    )(place, lines, *tables)


def halo(slabs):
    def shifted(piece, axis, up):
        devices = lax.axis_size(axis)
        pairs = [(i, i + 1) for i in range(devices - 1)]
        if not up:
            pairs = [(j, i) for i, j in pairs]
        return lax.ppermute(piece, axis, pairs)

    last_rows, first_rows, last_cols, first_cols = slabs
    return (
        shifted(last_rows, "px", True),
        shifted(first_rows, "px", False),
        shifted(last_cols, "py", True),
        shifted(first_cols, "py", False),
    )


def stretch(field, flow, halos, size):
    rows, cols, G = size.rows, size.cols, size.G
    width = 2 * G
    step = 16

    def kernel(field_ref, flow_ref, up_ref, down_ref, left_ref, right_ref, out_ref, ext_ref):
        for c in range(3):
            ext_ref[c, SUB : SUB + rows, 0:width] = left_ref[c]
            ext_ref[c, SUB : SUB + rows, width : width + cols * G] = flow_ref[c]
            ext_ref[c, SUB : SUB + rows, width + cols * G :] = right_ref[c]
            ext_ref[c, SUB - 2 : SUB, width : width + cols * G] = up_ref[c]
            ext_ref[c, SUB + rows : SUB + rows + 2, width : width + cols * G] = down_ref[c]
        depth = lax.broadcasted_iota(jnp.int32, (step, width), 1) % G
        inside = {s: (depth + s >= 0) & (depth + s < G) for s in (-2, -1, 1, 2)}

        def combine(p1, m1, p2, m2):
            return (8.0 * (p1 - m1) - (p2 - m2)) * (1.0 / 12.0)

        def block(b, _):
            at = pl.multiple_of(b * width, LANES)
            here_at = pl.multiple_of((b + 1) * width, LANES)
            for r in range(rows // step):
                fields = [field_ref[d, r * step : (r + 1) * step, pl.ds(at, width)] for d in range(3)]
                for c in range(3):
                    top = SUB + r * step
                    window = ext_ref[c, top : top + step, pl.ds(at, 3 * width)]
                    here = window[:, width : 2 * width]

                    def depth_shift(s):
                        return jnp.where(inside[s], pltpu.roll(here, (-s) % width, 1), 0.0)

                    def row_shift(s):
                        return ext_ref[c, top + s : top + s + step, pl.ds(here_at, width)]

                    total = fields[2] * combine(
                        depth_shift(1), depth_shift(-1), depth_shift(2), depth_shift(-2)
                    )
                    total += fields[1] * combine(
                        window[:, 3 * G : 5 * G],
                        window[:, G : 3 * G],
                        window[:, 4 * G :],
                        window[:, : 2 * G],
                    )
                    total += fields[0] * combine(
                        row_shift(1), row_shift(-1), row_shift(2), row_shift(-2)
                    )
                    out_ref[c, r * step : (r + 1) * step, pl.ds(at, width)] = total
            return 0

        lax.fori_loop(0, cols // 2, block, 0)

    return pl.pallas_call(
        kernel,
        out_shape=jax.ShapeDtypeStruct(flow.shape, f32),
        scratch_shapes=[pltpu.VMEM((3, rows + 2 * SUB, cols * G + 2 * width), f32)],
        cost_estimate=pl.CostEstimate(
            flops=60 * flow.size, bytes_accessed=12 * flow.size, transcendentals=0
        ),
        name="stretch",
    )(field, flow, *halos)


def triple(table, axis):
    high, low = split_table(table)
    return np.concatenate([high, high, low], axis=axis)


def fast(vorticity, size):
    rows, cols, G, devices, groups = size.rows, size.cols, size.G, size.devices, size.groups
    length, bands, others = size.length, size.bands, size.G // size.cols
    axes = ("px", "py")
    place = lax.axis_index(axes).astype(jnp.int32)

    cells = np.array([
        q * cols + band * SUB + s for band in range(bands) for q in range(others) for s in range(SUB)
    ])
    lane_modes, lane_kinds = lane_order(G)
    row_modes = np.concatenate([np.arange(G)] * 2)
    row_kinds = np.repeat([0, 1], G)
    line_basis = basis(G, lane_modes, lane_kinds, length)[cells]
    wide_basis = basis(G, row_modes, row_kinds, length)
    line = np.stack(split_table(line_basis))
    wide = triple(wide_basis.T, 1)
    inv_wide = triple(wide_basis * weights(row_modes, length), 1)
    inv_line = triple(line_basis * weights(lane_modes, length), 1)
    kx = np.broadcast_to(waves(np.arange(G), length)[:, None], (G, LANES)).astype(np.float32)
    signs = np.where(lane_kinds == 0, 1.0, -1.0)
    signs[: 2 * (G // LANES * LANES)] = 1.0
    ky = np.broadcast_to((waves(lane_modes, length) * signs)[None, :], (8, length)).astype(np.float32)
    tables = tuple(jnp.asarray(t) for t in (line, wide, inv_wide, inv_line, kx, ky))

    def depth_tables(start, kept):
        modes = np.array([
            (start + j) * devices + d
            for j in range(kept) for k in (0, 1) for d in range(devices)
        ])
        kinds = np.array([k for j in range(kept) for k in (0, 1) for d in range(devices)])
        table = basis(G, modes, kinds, length)
        forward = np.stack(split_table(table.T))
        inverse = np.stack(split_table((table * weights(modes, length)).T))
        return jnp.asarray(forward), jnp.asarray(inverse)

    def exchange(value, kept):
        value = value.reshape(devices, size.tiles(kept) * SUB, LANES)
        return lax.all_to_all(value, axes, split_axis=0, concat_axis=0, tiled=True)

    arrived = []
    for start, kept in size.chunks:
        sent = depth_forward(vorticity, depth_tables(start, kept)[0], size, kept)
        arrived.append(exchange(sent, kept))
    returned = []
    for (start, kept), lines in zip(size.chunks, arrived):
        lines = lines.reshape(groups, others, size.tiles(kept), SUB, LANES)
        where = jnp.stack([place, jnp.int32(start)])
        returned.append(exchange(planes(lines, where, tables, size, kept), kept))
    flow, slabs = None, None
    for (start, kept), lines in zip(size.chunks, returned):
        last = start + kept == G // devices
        flow, *slabs = depth_inverse(
            lines.reshape(-1, LANES), depth_tables(start, kept)[1], flow, size, kept, last
        )
    return flow, stretch(vorticity, flow, halo(slabs), size)


def with_halo(shard, sides, width):
    for axis, dim in sides:
        devices, length = (lax.axis_size(axis), shard.shape[dim])
        up = [(i, (i + 1) % devices) for i in range(devices - 1)]
        down = [(j, i) for i, j in up]
        last = lax.slice_in_dim(shard, length - width, length, axis=dim)
        leading = lax.slice_in_dim(shard, 0, width, axis=dim)
        before = lax.ppermute(last, axis, up)
        after = lax.ppermute(leading, axis, down)
        shard = jnp.concatenate([before, shard, after], axis=dim)
    return shard


def twiddle(count_in, count_out, length, factor):
    source = lax.broadcasted_iota(jnp.int32, (count_in, count_out), 0)
    target = lax.broadcasted_iota(jnp.int32, (count_in, count_out), 1)
    angle = (source * target % length).astype(jnp.float32) * (2.0 * math.pi / length)
    cosine = jnp.cos(angle) * factor
    sine = jnp.sin(angle) * factor
    return (
        jnp.broadcast_to(cosine, (3, count_in, count_out)),
        jnp.broadcast_to(sine, (3, count_in, count_out)),
    )


def product(einsum_form, first, second):
    return jnp.einsum(einsum_form, first, second, precision=highest)


def forward_left(pair, einsum_form, tables):
    real_part, imag_part = pair
    cosine_table, sine_table = tables
    return (
        product(einsum_form, cosine_table, real_part) + product(einsum_form, sine_table, imag_part),
        product(einsum_form, cosine_table, imag_part) - product(einsum_form, sine_table, real_part),
    )


def forward_right(pair, einsum_form, tables):
    real_part, imag_part = pair
    cosine_table, sine_table = tables
    return (
        product(einsum_form, real_part, cosine_table) + product(einsum_form, imag_part, sine_table),
        product(einsum_form, imag_part, cosine_table) - product(einsum_form, real_part, sine_table),
    )


def backward_left(pair, einsum_form, tables):
    real_part, imag_part = pair
    cosine_table, sine_table = tables
    return (
        product(einsum_form, cosine_table, real_part) - product(einsum_form, sine_table, imag_part),
        product(einsum_form, cosine_table, imag_part) + product(einsum_form, sine_table, real_part),
    )


def wavenumbers(start, count, length, position):
    index = start + lax.iota(jnp.int32, count)
    signed = jnp.where(index < length // 2, index, index - length)
    wave = signed.astype(jnp.float32) * (2.0 * math.pi / length)
    slope = jnp.where(index == length // 2, 0.0, wave)
    keep = jnp.where(index == length // 2, 0.0, 1.0)
    shape = [1, 1, 1, 1]
    shape[position] = count
    return (wave.reshape(shape), slope.reshape(shape), keep.reshape(shape))


def velocity_spectrum(pair, waves_x, waves_y, waves_z):
    square = waves_x[0] ** 2 + waves_y[0] ** 2 + waves_z[0] ** 2
    mask = waves_x[2] * waves_y[2] * waves_z[2]
    green = (
        mask
        * jnp.exp(-0.5 * smoothing * smoothing * square)
        / (square + jnp.where(square == 0.0, 1.0, 0.0))
    )
    slope_x, slope_y, slope_z = (waves_x[1][0], waves_y[1][0], waves_z[1][0])

    def curl(field):
        return jnp.stack(
            [
                slope_y * field[2] - slope_z * field[1],
                slope_z * field[0] - slope_x * field[2],
                slope_x * field[1] - slope_y * field[0],
            ]
        )

    real_part = pair[0] * green
    imag_part = pair[1] * green
    return (jnp.swapaxes(-curl(imag_part), 1, 2), jnp.swapaxes(curl(real_part), 1, 2))


def window(padded, axis, offset):
    starts = [0, 2, 2, 2]
    limits = [padded.shape[0], padded.shape[1] - 2, padded.shape[2] - 2, padded.shape[3] - 2]
    starts[axis] = starts[axis] + offset
    limits[axis] = limits[axis] + offset
    return lax.slice(padded, starts, limits)


def derivative(padded, axis):
    near = window(padded, axis, 1) - window(padded, axis, -1)
    far = window(padded, axis, 2) - window(padded, axis, -2)
    return (8.0 * near - far) / 12.0


def general(vorticity):
    block_rows = vorticity.shape[1]
    G = block_rows * lax.axis_size("px")
    block_cols = vorticity.shape[2] // G
    field = vorticity.reshape(3, block_rows, block_cols, G)
    length = 2 * G
    depth_tables = twiddle(G, G, length, 1.0)
    line_tables = twiddle(G, length, length, 1.0)
    inverse_tables = twiddle(length, G, length, 1.0 / length)
    closing = twiddle(G, G, length, 1.0 / length)
    weights = jnp.where(lax.iota(jnp.int32, G) == 0, 1.0, 2.0)[None, :, None]
    closing_cos = closing[0] * weights
    closing_sin = closing[1] * weights
    pair = (
        product("czk,cxyz->ckxy", depth_tables[0], field),
        -product("czk,cxyz->ckxy", depth_tables[1], field),
    )
    pair = (
        lax.all_to_all(pair[0], "py", split_axis=1, concat_axis=3, tiled=True),
        lax.all_to_all(pair[1], "py", split_axis=1, concat_axis=3, tiled=True),
    )
    pair = forward_left(pair, "cyl,ckxy->clkx", line_tables)
    pair = (
        lax.all_to_all(pair[0], "px", split_axis=1, concat_axis=3, tiled=True),
        lax.all_to_all(pair[1], "px", split_axis=1, concat_axis=3, tiled=True),
    )
    pair = forward_right(pair, "clkx,cxm->clkm", line_tables)
    rows = pair[0].shape[1]
    depth = pair[0].shape[2]
    waves_y = wavenumbers(lax.axis_index("px") * rows, rows, length, 1)
    waves_z = wavenumbers(lax.axis_index("py") * depth, depth, length, 2)
    waves_x = wavenumbers(0, length, length, 3)
    pair = velocity_spectrum(pair, waves_x, waves_y, waves_z)
    pair = backward_left(pair, "cmx,cklm->cxkl", inverse_tables)
    pair = (
        lax.all_to_all(pair[0], "px", split_axis=1, concat_axis=3, tiled=True),
        lax.all_to_all(pair[1], "px", split_axis=1, concat_axis=3, tiled=True),
    )
    pair = backward_left(pair, "cly,cxkl->cyxk", inverse_tables)
    pair = (
        lax.all_to_all(pair[0], "py", split_axis=1, concat_axis=3, tiled=True),
        lax.all_to_all(pair[1], "py", split_axis=1, concat_axis=3, tiled=True),
    )
    flow = product("cyxk,ckz->cyxz", pair[0], closing_cos) - product(
        "cyxk,ckz->cyxz", pair[1], closing_sin
    )
    flow = jnp.swapaxes(flow, 1, 2)
    padded = with_halo(flow, (("px", 1), ("py", 2)), 2)
    padded = jnp.pad(padded, ((0, 0), (0, 0), (0, 0), (2, 2)))
    stretching = (
        field[0] * derivative(padded, 1)
        + field[1] * derivative(padded, 2)
        + field[2] * derivative(padded, 3)
    )
    return (
        flow.reshape(3, block_rows, block_cols * G),
        stretching.reshape(3, block_rows, block_cols * G),
    )


def on_device(vorticity):
    sizes = fast_sizes(vorticity)
    return general(vorticity) if sizes is None else fast(vorticity, sizes)


def solution(mesh):
    in_specs = (P(None, "px", "py"),)
    out_specs = (P(None, "px", "py"), P(None, "px", "py"))
    return jax.shard_map(
        on_device, mesh=mesh, in_specs=in_specs, out_specs=out_specs, check_vma=False
    )
```

time: 321 us -> 316 us (0.984)
  waiting for transfers between devices: 186 us -> 171 us
  Pallas kernels: 95.1 us -> 106 us
    all_to_all x4, waiting for transfers between devices: 183 us -> 164 us  [exchange(): return lax.all_to_all(value, axes, split_axis=0, concat_axis=0, tiled=True)]
    pallas_call x2, Pallas kernels: 54.1 us -> 59.6 us  [planes(): pl.pallas_call(kernel, out_shape=jax.ShapeDtypeStruct(lines.shape, f32),...]
    ppermute x4, waiting for transfers between devices: 2.95 us -> 6.73 us  [shifted(): return lax.ppermute(piece, axis, pairs)]
    ppermute x4, starting transfers between devices: 10.2 us -> 6.84 us  [shifted(): return lax.ppermute(piece, axis, pairs)]
    unnamed x14 -> x34, local copies, waits for them, and re-layouts: 5.99 us -> 8.77 us
  transfers between devices with their start and end apart: 8 -> 8, of which waited for: 6 -> 5; matrix products, arithmetic and copies ran while one was open for 0% -> 0% of each run, Pallas kernels for 21% -> 24%
where the time goes in v2:
time: 316 us; the launch traced here: 315 us
  waiting for transfers between devices  171 us (54%)
  Pallas kernels  106 us (34%)
  starting transfers between devices  28.5 us (9%)
  local copies, waits for them, and re-layouts  8.77 us (3%)
    all_to_all x4, waiting for transfers between devices, exchange(): return lax.all_to_all(value, axes, split_axis=0, concat_axis=0, tiled=True)  164 us
    pallas_call x2, Pallas kernels, planes(): pl.pallas_call(kernel, out_shape=jax.ShapeDtypeStruct(lines.shape, f32),...  59.6 us
    all_to_all x4, starting transfers between devices, exchange(): return lax.all_to_all(value, axes, split_axis=0, concat_axis=0, tiled=True)  21.6 us
    pallas_call x2, Pallas kernels, depth_inverse(): pl.pallas_call(kernel, out_shape=outs, scratch_shapes=[pltpu.VMEM((3 * bl...  16.7 us
    pallas_call x2, Pallas kernels, depth_forward(): pl.pallas_call(kernel, out_shape=jax.ShapeDtypeStruct((devices * tiles *...  15.5 us
    pallas_call x1, Pallas kernels, stretch(): pl.pallas_call(kernel, out_shape=jax.ShapeDtypeStruct(flow.shape, f32), s...  14.4 us
    unnamed x34, local copies, waits for them, and re-layouts  8.77 us
    ppermute x4, starting transfers between devices, shifted(): return lax.ppermute(piece, axis, pairs)  6.84 us
  transfers between devices with their start and end apart: 8, of which 5 were waited for; matrix products, arithmetic and copies ran while one was open for 0% of the time, Pallas kernels for 24%

profile of v2, /device:TPU:0, one launch (start us, length us, event | category | flops | bytes accessed | tf_op | source)
XLA Modules:
  0.0 315.2 jit_solution(13535595223838897529)
XLA Ops:
  0.6 8.7 %depth_forward.3 = f32[6912,128]{1,0:T(8,128)} custom-call(f32[3,48,4608]{2,1,0:T(8,128)} %field_ref.1, bf16[2,256,192]{2,1,0:T(8,128)(2,1)} %constant.40.clone.table_ref), custom_call_target="tpu_custom_call" | custom-call | flops 1019215872 | bytes 6193152 | tf_op jit(solution)/shard_map/depth_forward/pallas_call | solution.py:134
  9.3 7.3 %all-to-all-start.2 = ((f32[32,216,128]{2,1,0:T(8,128)}), f32[32,216,128]{2,1,0:T(8,128)S(1)}, u32[]{:S(2)}, u32[]{:S(2)}) async-start(f32[32,216,128]{2,1,0:T(8,128)} %bitcast.11), calls=%async_computation.2 | async-start | bytes 7077888 | tf_op jit(solution)/shard_map/all_to_all | solution.py:522
  16.6 6.8 %depth_forward.2 = f32[3584,128]{1,0:T(8,128)} custom-call(f32[3,48,4608]{2,1,0:T(8,128)} %field_ref.1, bf16[2,128,192]{2,1,0:T(8,128)(2,1)} %constant.41.clone.table_ref), custom_call_target="tpu_custom_call" | custom-call | flops 509607936 | bytes 4489216 | tf_op jit(solution)/shard_map/depth_forward/pallas_call | solution.py:134
  23.4 72.9 %all-to-all-done.2 = f32[32,216,128]{2,1,0:T(8,128)S(1)} async-done(((f32[32,216,128]{2,1,0:T(8,128)}), f32[32,216,128]{2,1,0:T(8,128)S(1)}, u32[]{:S(2)}, u32[]{:S(2)}) %all-to-all-start.2) | async-done | bytes 3538976 | tf_op jit(solution)/shard_map/all_to_all | solution.py:522
  96.4 4.2 %all-to-all-start = ((f32[32,112,128]{2,1,0:T(8,128)}), f32[32,112,128]{2,1,0:T(8,128)}, u32[]{:S(2)}, u32[]{:S(2)}) async-start(f32[32,112,128]{2,1,0:T(8,128)} %bitcast.12), calls=%async_computation | async-start | bytes 3670016 | tf_op jit(solution)/shard_map/all_to_all | solution.py:522
  100.6 1.0 copy-done.1
  101.7 1.0 copy-done.3
  105.5 36.9 %planes.3 = f32[4,8,27,8,128]{4,3,2,1,0:T(8,128)S(1)} custom-call(s32[2]{0:T(128)S(1)} %pad_add_fusion.1.place_ref, f32[4,8,27,8,128]{4,3,2,1,0:T(8,128)S(1)} %bitcast.9, bf16[2,192,384]{2,1,0:T(8,128)(2,1)S(1)} %copy-done.7, bf16[384,576]{1,0:T(8,128)(2,1)S(1)} %copy-done.1, bf16[192,1152]{1,0:T(8,128)(2,1)S(1)} %copy-done.3, ...), custom_call_target="tpu_custom_call" | custom-call | flops 24461180928 | bytes 7077888 | tf_op jit(solution)/shard_map/planes/pallas_call | solution.py:382
  142.4 1.8 copy-done
  144.2 5.9 %all-to-all-start.3 = ((f32[32,216,128]{2,1,0:T(8,128)}), f32[32,216,128]{2,1,0:T(8,128)}, u32[]{:S(2)}, u32[]{:S(2)}) async-start(f32[32,216,128]{2,1,0:T(8,128)} %bitcast.10), calls=%async_computation.3 | async-start | bytes 7077888 | tf_op jit(solution)/shard_map/all_to_all | solution.py:522
  150.2 22.7 %planes.2 = f32[4,8,14,8,128]{4,3,2,1,0:T(8,128)} custom-call(s32[2]{0:T(128)S(1)} %pad_add_fusion.place_ref, f32[4,8,14,8,128]{4,3,2,1,0:T(8,128)} %bitcast.2.lines_ref, bf16[2,192,384]{2,1,0:T(8,128)(2,1)S(1)} %copy-done.8, bf16[384,576]{1,0:T(8,128)(2,1)S(1)} %copy-done.2, bf16[192,1152]{1,0:T(8,128)(2,1)S(1)} %copy-done.4, ...), custom_call_target="tpu_custom_call" | custom-call | flops 12230590464 | bytes 3670016 | tf_op jit(solution)/shard_map/planes/pallas_call | solution.py:382
  173.0 56.9 %all-to-all-done.3 = f32[32,216,128]{2,1,0:T(8,128)} async-done(((f32[32,216,128]{2,1,0:T(8,128)}), f32[32,216,128]{2,1,0:T(8,128)}, u32[]{:S(2)}, u32[]{:S(2)}) %all-to-all-start.3) | async-done | bytes 3538976 | tf_op jit(solution)/shard_map/all_to_all | solution.py:522
  229.9 4.2 %all-to-all-start.1 = ((f32[32,112,128]{2,1,0:T(8,128)}), f32[32,112,128]{2,1,0:T(8,128)S(1)}, u32[]{:S(2)}, u32[]{:S(2)}) async-start(f32[32,112,128]{2,1,0:T(8,128)} %bitcast.3), calls=%async_computation.1 | async-start | bytes 3670016 | tf_op jit(solution)/shard_map/all_to_all | solution.py:522
  234.1 8.7 %depth_inverse.2.refs_0_ = f32[3,48,4608]{2,1,0:T(8,128)} custom-call(f32[6912,128]{1,0:T(8,128)} %bitcast.8.lines_ref, bf16[2,256,192]{2,1,0:T(8,128)(2,1)} %constant.42.clone.table_ref), custom_call_target="tpu_custom_call" | custom-call | flops 1019215872 | bytes 8847360 | tf_op jit(solution)/shard_map/depth_inverse/pallas_call | solution.py:210
  242.8 34.4 %all-to-all-done.1 = f32[32,112,128]{2,1,0:T(8,128)S(1)} async-done(((f32[32,112,128]{2,1,0:T(8,128)}), f32[32,112,128]{2,1,0:T(8,128)S(1)}, u32[]{:S(2)}, u32[]{:S(2)}) %all-to-all-start.1) | async-done | bytes 1835040 | tf_op jit(solution)/shard_map/all_to_all | solution.py:522
  277.2 1.2 copy-done.12
  278.4 8.0 %depth_inverse.3 = (f32[3,48,4608]{2,1,0:T(8,128)}, f32[3,2,4608]{2,1,0:T(2,128)}, f32[3,2,4608]{2,1,0:T(2,128)}, f32[3,48,384]{2,1,0:T(8,128)}, f32[3,48,384]{2,1,0:T(8,128)}) custom-call(f32[3584,128]{1,0:T(8,128)} %bitcast.13, bf16[2,128,192]{2,1,0:T(8,128)(2,1)} %constant.43.clone.table_ref, f32[3,48,4608]{2,1,0:T(8,128)} %depth_inverse.2.refs_0_), custom_call_target="tpu_custom_call" | custom-call | flops 509607936 | bytes 7143424 | tf_op jit(solution)/shard_map/depth_inverse/pallas_call | solution.py:210
  286.4 1.4 collective-permute-start.2
  287.9 1.3 collective-permute-start.3
  289.2 2.8 collective-permute-start
  292.0 1.3 collective-permute-start.1
  293.3 2.2 collective-permute-done.up_ref
  295.5 4.6 %collective-permute-done.1.down_ref = f32[3,2,4608]{2,1,0:T(2,128)S(1)} collective-permute-done((f32[3,2,4608]{2,1,0:T(2,128)}, f32[3,2,4608]{2,1,0:T(2,128)S(1)}, u32[]{:S(2)}, u32[]{:S(2)}) %collective-permute-start.1) | collective-permute-done | bytes 110624 | tf_op jit(solution)/shard_map/ppermute | solution.py:407
  300.9 14.4 %stretch.1 = f32[3,48,4608]{2,1,0:T(8,128)} custom-call(f32[3,48,4608]{2,1,0:T(8,128)} %field_ref.1, f32[3,48,4608]{2,1,0:T(8,128)} %get-tuple-element.5.flow_ref, f32[3,2,4608]{2,1,0:T(2,128)} %copy-done.15, f32[3,2,4608]{2,1,0:T(2,128)} %copy-done.16, f32[3,48,384]{2,1,0:T(8,128)} %copy-done.13, f32[3,48,384]{2,1,0:T(8,128)} %copy-done.14), custom_call_target="tpu_custom_call" | custom-call | flops 39813120 | bytes 7962624 | tf_op jit(solution)/shard_map/stretch/pallas_call | solution.py:469
  (35 shorter events, 3.9 us)
Async XLA Ops:
  9.3 87.1 %all-to-all-start.2 = ((f32[32,216,128]{2,1,0:T(8,128)}), f32[32,216,128]{2,1,0:T(8,128)S(1)}, u32[]{:S(2)}, u32[]{:S(2)}) async-start(f32[32,216,128]{2,1,0:T(8,128)} %bitcast.11), calls=%async_computation.2 | async-start | bytes 7077888 | tf_op jit(solution)/shard_map/all_to_all | solution.py:522
  23.4 77.2 %copy-start.11 = (f32[8,384]{1,0:T(8,128)S(1)}, f32[8,384]{1,0:T(8,128)}, u32[]{:S(2)}) copy-start(f32[8,384]{1,0:T(8,128)} %constant.39.clone.ky_ref) | copy-start | bytes 36868
  96.4 47.9 %all-to-all-start = ((f32[32,112,128]{2,1,0:T(8,128)}), f32[32,112,128]{2,1,0:T(8,128)}, u32[]{:S(2)}, u32[]{:S(2)}) async-start(f32[32,112,128]{2,1,0:T(8,128)} %bitcast.12), calls=%async_computation | async-start | bytes 3670016 | tf_op jit(solution)/shard_map/all_to_all | solution.py:522
  100.6 1.0 copy-start.1
  101.7 1.0 copy-start.3
  102.7 1.0 copy-start.5
  103.7 1.0 copy-start.7
  104.6 0.9 copy-start.9
  142.4 1.8 copy-start
  144.2 6.0 %copy-start.2 = (bf16[384,576]{1,0:T(8,128)(2,1)S(1)}, bf16[384,576]{1,0:T(8,128)(2,1)}, u32[]{:S(2)}) copy-start(bf16[384,576]{1,0:T(8,128)(2,1)} %constant.35.clone.wide_ref) | copy-start | bytes 1327108
  144.2 6.0 %copy-start.4 = (bf16[192,1152]{1,0:T(8,128)(2,1)S(1)}, bf16[192,1152]{1,0:T(8,128)(2,1)}, u32[]{:S(2)}) copy-start(bf16[192,1152]{1,0:T(8,128)(2,1)} %constant.36.clone.inv_wide_ref) | copy-start | bytes 1327108
  144.2 6.0 %copy-start.6 = (bf16[192,1152]{1,0:T(8,128)(2,1)S(1)}, bf16[192,1152]{1,0:T(8,128)(2,1)}, u32[]{:S(2)}) copy-start(bf16[192,1152]{1,0:T(8,128)(2,1)} %constant.37.clone.inv_line_ref) | copy-start | bytes 1327108
  144.2 6.0 %copy-start.8 = (bf16[2,192,384]{2,1,0:T(8,128)(2,1)S(1)}, bf16[2,192,384]{2,1,0:T(8,128)(2,1)}, u32[]{:S(2)}) copy-start(bf16[2,192,384]{2,1,0:T(8,128)(2,1)} %constant.34.clone.line_ref) | copy-start | bytes 884740
  144.2 6.0 %copy-start.10 = (f32[192,128]{1,0:T(8,128)S(1)}, f32[192,128]{1,0:T(8,128)}, u32[]{:S(2)}) copy-start(f32[192,128]{1,0:T(8,128)} %constant.38.clone.kx_ref) | copy-start | bytes 294916
  144.2 85.6 %all-to-all-start.3 = ((f32[32,216,128]{2,1,0:T(8,128)}), f32[32,216,128]{2,1,0:T(8,128)}, u32[]{:S(2)}, u32[]{:S(2)}) async-start(f32[32,216,128]{2,1,0:T(8,128)} %bitcast.10), calls=%async_computation.3 | async-start | bytes 7077888 | tf_op jit(solution)/shard_map/all_to_all | solution.py:522
  229.9 47.3 %all-to-all-start.1 = ((f32[32,112,128]{2,1,0:T(8,128)}), f32[32,112,128]{2,1,0:T(8,128)S(1)}, u32[]{:S(2)}, u32[]{:S(2)}) async-start(f32[32,112,128]{2,1,0:T(8,128)} %bitcast.3), calls=%async_computation.1 | async-start | bytes 3670016 | tf_op jit(solution)/shard_map/all_to_all | solution.py:522
  277.2 1.2 copy-start.12
  286.4 13.6 %collective-permute-start.2 = (f32[3,48,384]{2,1,0:T(8,128)}, f32[3,48,384]{2,1,0:T(8,128)S(1)}, u32[]{:S(2)}, u32[]{:S(2)}) collective-permute-start(f32[3,48,384]{2,1,0:T(8,128)} %get-tuple-element.10), channel_id=1, source_target_pairs={{0,1},{1,2},{2,3},{3,4},{4,5},{5,6},{6,7},{8,9},{9,10},{10,11},{11... | collective-permute-start | bytes 663560 | tf_op jit(solution)/shard_map/ppermute | solution.py:407
  287.9 12.2 %collective-permute-start.3 = (f32[3,48,384]{2,1,0:T(8,128)}, f32[3,48,384]{2,1,0:T(8,128)S(1)}, u32[]{:S(2)}, u32[]{:S(2)}) collective-permute-start(f32[3,48,384]{2,1,0:T(8,128)} %get-tuple-element.11), channel_id=1, source_target_pairs={{1,0},{2,1},{3,2},{4,3},{5,4},{6,5},{7,6},{9,8},{10,9},{11,10},{12... | collective-permute-start | bytes 663560 | tf_op jit(solution)/shard_map/ppermute | solution.py:407
  289.2 6.3 %collective-permute-start = (f32[3,2,4608]{2,1,0:T(2,128)}, f32[3,2,4608]{2,1,0:T(2,128)S(1)}, u32[]{:S(2)}, u32[]{:S(2)}) collective-permute-start(f32[3,2,4608]{2,1,0:T(2,128)} %get-tuple-element.8), channel_id=1, source_target_pairs={{0,8},{8,16},{16,24},{1,9},{9,17},{17,25},{2,10},{10,18},{18,26},{... | collective-permute-start | bytes 331784 | tf_op jit(solution)/shard_map/ppermute | solution.py:407
  292.0 8.0 %collective-permute-start.1 = (f32[3,2,4608]{2,1,0:T(2,128)}, f32[3,2,4608]{2,1,0:T(2,128)S(1)}, u32[]{:S(2)}, u32[]{:S(2)}) collective-permute-start(f32[3,2,4608]{2,1,0:T(2,128)} %get-tuple-element.9), channel_id=1, source_target_pairs={{8,0},{16,8},{24,16},{9,1},{17,9},{25,17},{10,2},{18,10},{26,18},{... | collective-permute-start | bytes 331784 | tf_op jit(solution)/shard_map/ppermute | solution.py:407
  295.5 4.6 %copy-start.15 = (f32[3,2,4608]{2,1,0:T(2,128)}, f32[3,2,4608]{2,1,0:T(2,128)S(1)}, u32[]{:S(2)}) copy-start(f32[3,2,4608]{2,1,0:T(2,128)S(1)} %collective-permute-done.up_ref) | copy-start | bytes 331780
  300.0 0.7 copy-start.13
  300.0 0.8 copy-start.14
  (1 other events, 0.6 us)

commit v3 on v2

--- a/solution.py
+++ b/solution.py
@@ -7,6 +7,7 @@
 from jax.experimental import pallas as pl
 from jax.experimental.pallas import tpu as pltpu
 from jax.sharding import PartitionSpec as P
+
 
 smoothing = 1.0
 highest = lax.Precision.HIGHEST
@@ -57,7 +58,6 @@
 
 NN = ((1,), (0,))
 NT = ((1,), (1,))
-TN = ((0,), (0,))
 
 
 def halves(value):
@@ -73,14 +73,14 @@
         self.bands = cols // SUB
         self.length = 2 * G
         total = G // devices
-        first = max(1, total * 2 // 3)
+        first = max(1, total // 3)
         self.chunks = [(0, first), (first, total - first)] if total > first else [(0, first)]
 
-    def units(self, kept):
-        return 6 * kept
-
-    def tiles(self, kept):
-        return -(-self.bands * self.units(kept) * self.rows // LANES)
+    def units(self, kept, count=3):
+        return 2 * count * kept
+
+    def tiles(self, kept, count=3):
+        return -(-self.bands * self.units(kept, count) * self.rows // LANES)
 
 
 def fast_sizes(vorticity):
@@ -148,15 +148,19 @@
     )(shard, table)
 
 
-def depth_inverse(lines, table, before, size, kept, slabs):
+def depth_inverse(lines, table, before, size, kept, parts, slabs):
     rows, cols, G, devices = size.rows, size.cols, size.G, size.devices
-    units, tiles, bands = size.units(kept), size.tiles(kept), size.bands
+    start, count = parts
+    units, tiles, bands = size.units(kept, count), size.tiles(kept, count), size.bands
     block = 2 * kept * devices
+    own = pl.BlockSpec((count, rows, cols * G), lambda i: (start // count, 0, 0))
+    whole = pl.BlockSpec(memory_space=pltpu.VMEM)
     extra = [] if before is None else [before]
     outs = [jax.ShapeDtypeStruct((3, rows, cols * G), f32)]
     if slabs:
-        outs += [jax.ShapeDtypeStruct((3, 2, cols * G), f32)] * 2
-        outs += [jax.ShapeDtypeStruct((3, rows, 2 * G), f32)] * 2
+        outs += [jax.ShapeDtypeStruct((count, 2, cols * G), f32)] * 2
+        outs += [jax.ShapeDtypeStruct((count, rows, 2 * G), f32)] * 2
+        outs += [jax.ShapeDtypeStruct((count, rows, cols * G), f32)]
 
     def kernel(lines_ref, table_ref, *refs):
         before_ref = refs[0] if before is not None else None
@@ -199,31 +203,36 @@
                 if slabs:
                     slab_refs[0][c, :, y * G : (y + 2) * G] = pair[rows - 2 :, :]
                     slab_refs[1][c, :, y * G : (y + 2) * G] = pair[:2, :]
+                    slab_refs[4][c, :, y * G : (y + 2) * G] = pair
                 if slabs and y == cols - 2:
                     slab_refs[2][c] = pair
                 if slabs and y == 0:
                     slab_refs[3][c] = pair
             return 0
 
-        lax.fori_loop(0, 3, component, 0)
+        lax.fori_loop(0, count, component, 0)
 
     return pl.pallas_call(
         kernel,
+        grid=(1,),
         out_shape=outs,
+        in_specs=[whole, whole] + [own] * len(extra),
+        out_specs=[own] + [whole] * (len(outs) - 1),
+        input_output_aliases={2: 0} if extra else {},
         scratch_shapes=[
-            pltpu.VMEM((3 * block, rows * cols), f32),
+            pltpu.VMEM((count * block, rows * cols), f32),
             pltpu.VMEM((rows * cols, G), f32),
         ],
         cost_estimate=pl.CostEstimate(
-            flops=18 * block * G * rows * cols,
-            bytes_accessed=4 * (6 * rows * cols * G + devices * tiles * SUB * LANES),
+            flops=6 * count * block * G * rows * cols,
+            bytes_accessed=4 * (3 * count * rows * cols * G + devices * tiles * SUB * LANES),
             transcendentals=0,
         ),
         name="depth_inverse",
     )(lines, table, *extra)
 
 
-def planes(lines, place, tables, size, kept):
+def planes(lines, place, tables, size, kept, splits):
     rows, cols, G, devices, groups = size.rows, size.cols, size.G, size.devices, size.groups
     units, tiles, bands, length = size.units(kept), size.tiles(kept), size.bands, size.length
     width = units * rows
@@ -233,7 +242,9 @@
     others = G // cols
 
     def kernel(place_ref, lines_ref, line_ref, wide_ref, inv_wide_ref, inv_line_ref,
-               kx_ref, ky_ref, out_ref, left_ref, spec_ref, turned_ref, back_ref):
+               kx_ref, ky_ref, *refs):
+        out_refs, (left_ref, spec_ref, turned_ref, back_ref) = refs[: len(splits)], refs[len(splits) :]
+
         def arrive(p, _):
             flat = jnp.concatenate(
                 [lines_ref[p, :, t].reshape(others * SUB, LANES).T for t in range(tiles)], axis=0
@@ -362,17 +373,22 @@
         lax.fori_loop(0, kept, one_depth, 0)
 
         def leave(p, _):
-            done = dot(inv_line_ref[:, : 2 * length], back_ref[p], NT) + dot(
-                inv_line_ref[:, 2 * length :], back_ref[p, :, :length], NT
-            )
-            pieces = [
-                done[band * others * SUB : (band + 1) * others * SUB, :] for band in range(bands)
-            ]
-            if tiles * LANES > bands * width:
-                pieces += [jnp.zeros((others * SUB, tiles * LANES - bands * width), f32)]
-            line = jnp.concatenate(pieces, axis=1)
-            for t in range(tiles):
-                out_ref[p, :, t] = line[:, t * LANES : (t + 1) * LANES].reshape(others, SUB, LANES)
+            for out_ref, (start, count) in zip(out_refs, splits):
+                many, span = size.tiles(kept, count), size.units(kept, count) * rows
+                at = size.units(kept, start) * rows
+                done = dot(
+                    inv_line_ref[:, : 2 * length], back_ref[p, at : at + span, :], NT
+                ) + dot(inv_line_ref[:, 2 * length :], back_ref[p, at : at + span, :length], NT)
+                pieces = [
+                    done[band * others * SUB : (band + 1) * others * SUB, :] for band in range(bands)
+                ]
+                if many * LANES > bands * span:
+                    pieces += [jnp.zeros((others * SUB, many * LANES - bands * span), f32)]
+                line = jnp.concatenate(pieces, axis=1)
+                for t in range(many):
+                    out_ref[p, :, t] = line[:, t * LANES : (t + 1) * LANES].reshape(
+                        others, SUB, LANES
+                    )
             return 0
 
         lax.fori_loop(0, groups, leave, 0)
@@ -381,9 +397,12 @@
     flops = 6 * (4 * groups * width * G * length + 24 * kept * length * G * length)
     return pl.pallas_call(
         kernel,
-        out_shape=jax.ShapeDtypeStruct(lines.shape, f32),
+        out_shape=[
+            jax.ShapeDtypeStruct((groups, others, size.tiles(kept, count), SUB, LANES), f32)
+            for _, count in splits
+        ],
         in_specs=[pl.BlockSpec(memory_space=pltpu.SMEM)] + [vmem] * 7,
-        out_specs=vmem,
+        out_specs=[vmem] * len(splits),
         scratch_shapes=[
             pltpu.VMEM((kept, 2 * G, 6 * length), bf16),
             pltpu.VMEM((length, 6 * length), f32),
@@ -415,66 +434,109 @@
     )
 
 
-def stretch(field, flow, halos, size):
+def depth_weights(G):
+    width = 2 * G
+    at = np.arange(width) % G
+    out = np.zeros((width // LANES * 4, LANES), np.float32)
+    for i, (shift, weight) in enumerate(((1, 8.0), (-1, -8.0), (2, -1.0), (-2, 1.0))):
+        row = np.where((at + shift >= 0) & (at + shift < G), weight / 12.0, 0.0)
+        for k in range(width // LANES):
+            out[4 * k + i] = row[k * LANES : (k + 1) * LANES]
+    return out
+
+
+def stretch(field, flow, halos, before, size, parts):
     rows, cols, G = size.rows, size.cols, size.G
-    width = 2 * G
-    step = 16
-
-    def kernel(field_ref, flow_ref, up_ref, down_ref, left_ref, right_ref, out_ref, ext_ref):
-        for c in range(3):
-            ext_ref[c, SUB : SUB + rows, 0:width] = left_ref[c]
-            ext_ref[c, SUB : SUB + rows, width : width + cols * G] = flow_ref[c]
-            ext_ref[c, SUB : SUB + rows, width + cols * G :] = right_ref[c]
-            ext_ref[c, SUB - 2 : SUB, width : width + cols * G] = up_ref[c]
-            ext_ref[c, SUB + rows : SUB + rows + 2, width : width + cols * G] = down_ref[c]
-        depth = lax.broadcasted_iota(jnp.int32, (step, width), 1) % G
-        inside = {s: (depth + s >= 0) & (depth + s < G) for s in (-2, -1, 1, 2)}
-
-        def combine(p1, m1, p2, m2):
-            return (8.0 * (p1 - m1) - (p2 - m2)) * (1.0 / 12.0)
+    start, count = parts
+    span = 2 * G // LANES
+    many = cols * G // LANES
+    half = LANES // 2
+    extra = [] if before is None else [before]
+
+    def kernel(field_ref, flow_ref, up_ref, down_ref, left_ref, right_ref, weight_ref, *refs):
+        out_ref, ext_ref, mix_ref = refs[len(extra) :]
+        for t in range(many):
+            at = slice(t * LANES, (t + 1) * LANES)
+            ext_ref[span + t, SUB : SUB + rows, :] = flow_ref[0, :, at]
+            ext_ref[span + t, SUB - 2 : SUB, :] = up_ref[0, :, at]
+            ext_ref[span + t, SUB + rows : SUB + rows + 2, :] = down_ref[0, :, at]
+        for t in range(span):
+            at = slice(t * LANES, (t + 1) * LANES)
+            ext_ref[t, SUB : SUB + rows, :] = left_ref[0, :, at]
+            ext_ref[span + many + t, SUB : SUB + rows, :] = right_ref[0, :, at]
+        lane = lax.broadcasted_iota(jnp.int32, (rows, LANES), 1)
+
+        def mix(t, turned):
+            after = pltpu.roll(ext_ref[t + 1, SUB : SUB + rows, :], half, 1)
+            mix_ref[t] = jnp.where(lane < half, turned, after)
+            return after
+
+        lax.fori_loop(
+            0, many + 2 * span - 1, mix, pltpu.roll(ext_ref[0, SUB : SUB + rows, :], half, 1)
+        )
 
         def block(b, _):
-            at = pl.multiple_of(b * width, LANES)
-            here_at = pl.multiple_of((b + 1) * width, LANES)
-            for r in range(rows // step):
-                fields = [field_ref[d, r * step : (r + 1) * step, pl.ds(at, width)] for d in range(3)]
-                for c in range(3):
-                    top = SUB + r * step
-                    window = ext_ref[c, top : top + step, pl.ds(at, 3 * width)]
-                    here = window[:, width : 2 * width]
-
-                    def depth_shift(s):
-                        return jnp.where(inside[s], pltpu.roll(here, (-s) % width, 1), 0.0)
-
-                    def row_shift(s):
-                        return ext_ref[c, top + s : top + s + step, pl.ds(here_at, width)]
-
-                    total = fields[2] * combine(
-                        depth_shift(1), depth_shift(-1), depth_shift(2), depth_shift(-2)
-                    )
-                    total += fields[1] * combine(
-                        window[:, 3 * G : 5 * G],
-                        window[:, G : 3 * G],
-                        window[:, 4 * G :],
-                        window[:, : 2 * G],
-                    )
-                    total += fields[0] * combine(
-                        row_shift(1), row_shift(-1), row_shift(2), row_shift(-2)
-                    )
-                    out_ref[c, r * step : (r + 1) * step, pl.ds(at, width)] = total
+            base = span * (b + 1)
+            own = [ext_ref[base + k, SUB : SUB + rows, :] for k in range(span)]
+            moved = {
+                (k, s): pltpu.roll(own[k], (-s) % LANES, 1)
+                for k in range(span)
+                for s in (1, -1, 2, -2)
+            }
+            for k in range(span):
+                deep = 0.0
+                for i, s in enumerate((1, -1, 2, -2)):
+                    value = moved[k, s]
+                    if s > 0 and k + 1 < span:
+                        value = jnp.where(lane < LANES - s, value, moved[k + 1, s])
+                    if s < 0 and k > 0:
+                        value = jnp.where(lane >= -s, value, moved[k - 1, s])
+                    deep = deep + weight_ref[4 * k + i : 4 * k + i + 1, :] * value
+                t = base + k
+                side = 8.0 * (mix_ref[t + 1] - mix_ref[t - 2]) - (
+                    ext_ref[t + span, SUB : SUB + rows, :] - ext_ref[t - span, SUB : SUB + rows, :]
+                )
+                tall = 8.0 * (
+                    ext_ref[t, SUB + 1 : SUB + 1 + rows, :] - ext_ref[t, SUB - 1 : SUB - 1 + rows, :]
+                ) - (ext_ref[t, SUB + 2 : SUB + 2 + rows, :] - ext_ref[t, SUB - 2 : SUB - 2 + rows, :])
+                at = pl.ds(pl.multiple_of((span * b + k) * LANES, LANES), LANES)
+                out_ref[0, :, at] = field_ref[2, :, at] * deep + (1.0 / 12.0) * (
+                    field_ref[1, :, at] * side + field_ref[0, :, at] * tall
+                )
             return 0
 
         lax.fori_loop(0, cols // 2, block, 0)
+
+    def part(*shape):
+        return pl.BlockSpec((1,) + shape, lambda i: (i, 0, 0))
 
     return pl.pallas_call(
         kernel,
-        out_shape=jax.ShapeDtypeStruct(flow.shape, f32),
-        scratch_shapes=[pltpu.VMEM((3, rows + 2 * SUB, cols * G + 2 * width), f32)],
+        grid=(count,),
+        out_shape=jax.ShapeDtypeStruct((3, rows, cols * G), f32),
+        in_specs=[
+            pl.BlockSpec((3, rows, cols * G), lambda i: (0, 0, 0)),
+            part(rows, cols * G),
+            part(2, cols * G),
+            part(2, cols * G),
+            part(rows, 2 * G),
+            part(rows, 2 * G),
+            pl.BlockSpec((4 * span, LANES), lambda i: (0, 0)),
+        ]
+        + [pl.BlockSpec(memory_space=pl.ANY)] * len(extra),
+        out_specs=pl.BlockSpec((1, rows, cols * G), lambda i: (start + i, 0, 0)),
+        input_output_aliases={7: 0} if extra else {},
+        scratch_shapes=[
+            pltpu.VMEM((many + 2 * span, rows + 2 * SUB, LANES), f32),
+            pltpu.VMEM((many + 2 * span - 1, rows, LANES), f32),
+        ],
         cost_estimate=pl.CostEstimate(
-            flops=60 * flow.size, bytes_accessed=12 * flow.size, transcendentals=0
+            flops=60 * flow.size,
+            bytes_accessed=8 * flow.size + 4 * field.size,
+            transcendentals=0,
         ),
         name="stretch",
-    )(field, flow, *halos)
+    )(field, flow, *halos, jnp.asarray(depth_weights(G)), *extra)
 
 
 def triple(table, axis):
@@ -483,7 +545,7 @@
 
 
 def fast(vorticity, size):
-    rows, cols, G, devices, groups = size.rows, size.cols, size.G, size.devices, size.groups
+    cols, G, devices, groups = size.cols, size.G, size.devices, size.groups
     length, bands, others = size.length, size.bands, size.G // size.cols
     axes = ("px", "py")
     place = lax.axis_index(axes).astype(jnp.int32)
@@ -509,34 +571,39 @@
     def depth_tables(start, kept):
         modes = np.array([
             (start + j) * devices + d
-            for j in range(kept) for k in (0, 1) for d in range(devices)
+            for j in range(kept) for _ in range(2) for d in range(devices)
         ])
-        kinds = np.array([k for j in range(kept) for k in (0, 1) for d in range(devices)])
+        kinds = np.array([k for _ in range(kept) for k in (0, 1) for _ in range(devices)])
         table = basis(G, modes, kinds, length)
         forward = np.stack(split_table(table.T))
         inverse = np.stack(split_table((table * weights(modes, length)).T))
         return jnp.asarray(forward), jnp.asarray(inverse)
 
-    def exchange(value, kept):
-        value = value.reshape(devices, size.tiles(kept) * SUB, LANES)
+    def exchange(value):
+        value = value.reshape(devices, -1, LANES)
         return lax.all_to_all(value, axes, split_axis=0, concat_axis=0, tiled=True)
 
     arrived = []
     for start, kept in size.chunks:
-        sent = depth_forward(vorticity, depth_tables(start, kept)[0], size, kept)
-        arrived.append(exchange(sent, kept))
+        arrived.append(exchange(depth_forward(vorticity, depth_tables(start, kept)[0], size, kept)))
     returned = []
     for (start, kept), lines in zip(size.chunks, arrived):
+        last = start + kept == G // devices
+        splits = ((0, 2), (2, 1)) if last else ((0, 3),)
         lines = lines.reshape(groups, others, size.tiles(kept), SUB, LANES)
         where = jnp.stack([place, jnp.int32(start)])
-        returned.append(exchange(planes(lines, where, tables, size, kept), kept))
-    flow, slabs = None, None
-    for (start, kept), lines in zip(size.chunks, returned):
-        last = start + kept == G // devices
+        for parts, done in zip(splits, planes(lines, where, tables, size, kept, splits)):
+            done = exchange(done)
+            returned.append((start, kept, parts, last, done))
+    flow, stretching = None, None
+    for start, kept, parts, last, lines in returned:
         flow, *slabs = depth_inverse(
-            lines.reshape(-1, LANES), depth_tables(start, kept)[1], flow, size, kept, last
+            lines.reshape(-1, LANES), depth_tables(start, kept)[1], flow, size, kept, parts, last
         )
-    return flow, stretch(vorticity, flow, halo(slabs), size)
+        if last:
+            *slabs, own = slabs
+            stretching = stretch(vorticity, own, halo(slabs), stretching, size, parts)
+    return flow, stretching
 
 
 def with_halo(shard, sides, width):
@@ -706,7 +773,9 @@
 
 def on_device(vorticity):
     sizes = fast_sizes(vorticity)
-    return general(vorticity) if sizes is None else fast(vorticity, sizes)
+    if sizes is None:
+        return general(vorticity)
+    return fast(vorticity, sizes)
 
 
 def solution(mesh):

time: 316 us -> 324 us (1.025)
  waiting for transfers between devices: 171 us -> 92.2 us
  blocking collectives: 0 us -> 61.6 us
  Pallas kernels: 106 us -> 115 us
  local copies, waits for them, and re-layouts: 8.77 us -> 17.5 us
  starting transfers between devices: 28.5 us -> 33.7 us
    all_to_all x4, waiting for transfers between devices: 164 us -> 92.1 us  [exchange(): return lax.all_to_all(value, axes, split_axis=0, concat_axis=0, tiled=True)]
    all_to_all x0 -> x1, blocking collectives: none -> 61.6 us  [exchange(): return lax.all_to_all(value, axes, split_axis=0, concat_axis=0, tiled=True)]
    pallas_call x5 -> x7, Pallas kernels: 90.6 us -> 99.3 us  [the longest x2 58.6 us: planes(): pl.pallas_call(kernel, out_shape=[jax.ShapeDtypeStruct((groups, others, s...]
    unnamed x34 -> x48, local copies, waits for them, and re-layouts: 8.77 us -> 17.5 us
    ppermute x4 -> x8, starting transfers between devices: 6.84 us -> 15.2 us  [shifted(): return lax.ppermute(piece, axis, pairs)]
    ppermute x4 -> x8, waiting for transfers between devices: 6.73 us -> 0.02 us  [shifted(): return lax.ppermute(piece, axis, pairs)]
  transfers between devices with their start and end apart: 8 -> 12, of which waited for: 5 -> 3; matrix products, arithmetic and copies ran while one was open for 0% -> 0% of each run, Pallas kernels for 24% -> 31%
where the time goes in v3:
time: 324 us; the launch traced here: 321 us
  Pallas kernels  115 us (35%)
  waiting for transfers between devices  92.2 us (28%)
  blocking collectives  61.6 us (19%)
  starting transfers between devices  33.7 us (10%)
  local copies, waits for them, and re-layouts  17.5 us (5%)
    all_to_all x4, waiting for transfers between devices, exchange(): return lax.all_to_all(value, axes, split_axis=0, concat_axis=0, tiled=True)  92.1 us
    all_to_all x1, blocking collectives, exchange(): return lax.all_to_all(value, axes, split_axis=0, concat_axis=0, tiled=True)  61.6 us
    pallas_call x2, Pallas kernels, planes(): pl.pallas_call(kernel, out_shape=[jax.ShapeDtypeStruct((groups, others, s...  58.6 us
    pallas_call x2, Pallas kernels, stretch(): pl.pallas_call(kernel, grid=(count,), out_shape=jax.ShapeDtypeStruct((3,...  21.5 us
    pallas_call x3, Pallas kernels, depth_inverse(): pl.pallas_call(kernel, grid=(1,), out_shape=outs, in_specs=[whole, whole]...  19.3 us
    all_to_all x4, starting transfers between devices, exchange(): return lax.all_to_all(value, axes, split_axis=0, concat_axis=0, tiled=True)  18.5 us
    unnamed x48, local copies, waits for them, and re-layouts  17.5 us
    pallas_call x2, Pallas kernels, depth_forward(): pl.pallas_call(kernel, out_shape=jax.ShapeDtypeStruct((devices * tiles *...  15.5 us
  transfers between devices with their start and end apart: 12, of which 3 were waited for; matrix products, arithmetic and copies ran while one was open for 0% of the time, Pallas kernels for 31%

profile of v3, /device:TPU:0, one launch (start us, length us, event | category | flops | bytes accessed | tf_op | source)
XLA Modules:
  0.0 320.7 jit_solution(9976357195422326836)
XLA Ops:
  0.6 6.8 %depth_forward.3 = f32[3584,128]{1,0:T(8,128)} custom-call(f32[3,48,4608]{2,1,0:T(8,128)} %field_ref.3, bf16[2,128,192]{2,1,0:T(8,128)(2,1)} %constant.42.clone.table_ref), custom_call_target="tpu_custom_call" | custom-call | flops 509607936 | bytes 4489216 | tf_op jit(solution)/shard_map/depth_forward/pallas_call | solution.py:134
  7.4 7.3 %all-to-all-start.3 = ((f32[32,112,128]{2,1,0:T(8,128)}), f32[32,112,128]{2,1,0:T(8,128)S(1)}, u32[]{:S(2)}, u32[]{:S(2)}) async-start(f32[32,112,128]{2,1,0:T(8,128)} %bitcast.17), calls=%async_computation.3 | async-start | bytes 3670016 | tf_op jit(solution)/shard_map/all_to_all | solution.py:584
  14.8 8.7 %depth_forward.2 = f32[6912,128]{1,0:T(8,128)} custom-call(f32[3,48,4608]{2,1,0:T(8,128)} %field_ref.3, bf16[2,256,192]{2,1,0:T(8,128)(2,1)} %constant.43.clone.table_ref), custom_call_target="tpu_custom_call" | custom-call | flops 1019215872 | bytes 6193152 | tf_op jit(solution)/shard_map/depth_forward/pallas_call | solution.py:134
  23.4 34.4 %all-to-all-done.3 = f32[32,112,128]{2,1,0:T(8,128)S(1)} async-done(((f32[32,112,128]{2,1,0:T(8,128)}), f32[32,112,128]{2,1,0:T(8,128)S(1)}, u32[]{:S(2)}, u32[]{:S(2)}) %all-to-all-start.3) | async-done | bytes 1835040 | tf_op jit(solution)/shard_map/all_to_all | solution.py:584
  59.1 4.1 %all-to-all-start = ((f32[32,216,128]{2,1,0:T(8,128)}), f32[32,216,128]{2,1,0:T(8,128)S(1)}, u32[]{:S(2)}, u32[]{:S(2)}) async-start(f32[32,216,128]{2,1,0:T(8,128)} %bitcast.15), calls=%async_computation | async-start | bytes 7077888 | tf_op jit(solution)/shard_map/all_to_all | solution.py:584
  63.3 1.5 copy-done.2
  69.7 20.5 %planes.3 = f32[4,8,14,8,128]{4,3,2,1,0:T(8,128)S(1)} custom-call(s32[2]{0:T(128)S(1)} %pad_add_fusion.1.place_ref, f32[4,8,14,8,128]{4,3,2,1,0:T(8,128)S(1)} %bitcast.13, bf16[2,192,384]{2,1,0:T(8,128)(2,1)S(1)} %copy-done.10, bf16[384,576]{1,0:T(8,128)(2,1)S(1)} %copy-done.4, bf16[192,1152]{1,0:T(8,128)(2,1)S(1)} %copy-done.8, ...), custom_call_target="tpu_custom_call" | custom-call | flops 12230590464 | bytes 3670016 | tf_op jit(solution)/shard_map/planes/pallas_call | solution.py:398
  91.5 51.5 %all-to-all-done = f32[32,216,128]{2,1,0:T(8,128)S(1)} async-done(((f32[32,216,128]{2,1,0:T(8,128)}), f32[32,216,128]{2,1,0:T(8,128)S(1)}, u32[]{:S(2)}, u32[]{:S(2)}) %all-to-all-start) | async-done | bytes 3538976 | tf_op jit(solution)/shard_map/all_to_all | solution.py:584
  142.9 4.2 %all-to-all-start.4 = ((f32[32,112,128]{2,1,0:T(8,128)}), f32[32,112,128]{2,1,0:T(8,128)}, u32[]{:S(2)}, u32[]{:S(2)}) async-start(f32[32,112,128]{2,1,0:T(8,128)} %bitcast.14), calls=%async_computation.4 | async-start | bytes 3670016 | tf_op jit(solution)/shard_map/all_to_all | solution.py:584
  152.1 38.0 %planes.2 = (f32[4,8,18,8,128]{4,3,2,1,0:T(8,128)S(1)}, f32[4,8,9,8,128]{4,3,2,1,0:T(8,128)}) custom-call(s32[2]{0:T(128)S(1)} %pad_add_fusion.place_ref, f32[4,8,27,8,128]{4,3,2,1,0:T(8,128)S(1)} %bitcast.11, bf16[2,192,384]{2,1,0:T(8,128)(2,1)S(1)} %copy-done.11, bf16[384,576]{1,0:T(8,128)(2,1)S(1)} %copy-done.5, bf16[192,1152]{1,0:T(8,128)(2,1)S(1)} %copy-done.9, ...), custom_call_target="tpu_custom_call" | custom-call | flops 24461180928 | bytes 7077888 | tf_op jit(solution)/shard_map/planes/pallas_call | solution.py:398
  190.2 1.4 copy-done
  191.6 61.6 %all_to_all.25 = f32[32,144,128]{2,1,0:T(8,128)} all-to-all(f32[32,144,128]{2,1,0:T(8,128)} %bitcast.12), channel_id=1, replica_groups=mesh['px'=4,'py'=8] {'px','py'}, dimensions={0} | all-to-all | bytes 4718592 | tf_op jit(solution)/shard_map/all_to_all | solution.py:584
  253.1 2.8 all-to-all-start.1
  256.0 6.8 %depth_inverse.3.refs_0_ = f32[3,48,4608]{2,1,0:T(8,128)} custom-call(f32[3584,128]{1,0:T(8,128)} %bitcast.10.lines_ref, bf16[2,128,192]{2,1,0:T(8,128)(2,1)} %constant.44.clone.table_ref), custom_call_target="tpu_custom_call" | custom-call | flops 509607936 | bytes 9797632 | tf_op jit(solution)/shard_map/depth_inverse/pallas_call | solution.py:215
  262.8 7.8 %depth_inverse.4 = (f32[3,48,4608]{2,1,0:T(8,128)}, f32[2,2,4608]{2,1,0:T(2,128)}, f32[2,2,4608]{2,1,0:T(2,128)}, f32[2,48,384]{2,1,0:T(8,128)}, f32[2,48,384]{2,1,0:T(8,128)}, /*index=5*/f32[2,48,4608]{2,1,0:T(8,128)}) custom-call(f32[4608,128]{1,0:T(8,128)} %bitcast.16, ...), custom_call_target="tpu_custom_call", output_to_operand_aliasing={{0}: (2, {})} | custom-call | flops 679477248 | bytes 7667712 | tf_op jit(solution)/shard_map/depth_inverse/pallas_call | solution.py:215
  270.6 1.8 collective-permute-start.6
  273.7 3.6 %collective-permute-start.4 = (f32[2,2,4608]{2,1,0:T(2,128)}, f32[2,2,4608]{2,1,0:T(2,128)S(1)}, u32[]{:S(2)}, u32[]{:S(2)}) collective-permute-start(f32[2,2,4608]{2,1,0:T(2,128)} %get-tuple-element.26), channel_id=1, source_target_pairs={{0,8},{8,16},{16,24},{1,9},{9,17},{17,25},{2,10},{10,18},{18,26},{... | collective-permute-start | bytes 221192 | tf_op jit(solution)/shard_map/ppermute | solution.py:426
  277.3 1.3 collective-permute-start.5
  278.6 6.3 %all-to-all-done.1 = f32[32,72,128]{2,1,0:T(8,128)S(1)} async-done(((f32[32,72,128]{2,1,0:T(8,128)}), f32[32,72,128]{2,1,0:T(8,128)S(1)}, u32[]{:S(2)}, u32[]{:S(2)}) %all-to-all-start.1) | async-done | bytes 1179680 | tf_op jit(solution)/shard_map/all_to_all | solution.py:584
  285.9 4.7 %depth_inverse.5 = (f32[3,48,4608]{2,1,0:T(8,128)}, f32[1,2,4608]{2,1,0:T(2,128)}, f32[1,2,4608]{2,1,0:T(2,128)}, f32[1,48,384]{2,1,0:T(8,128)}, f32[1,48,384]{2,1,0:T(8,128)}, /*index=5*/f32[1,48,4608]{2,1,0:T(8,128)}) custom-call(f32[2304,128]{1,0:T(8,128)} %bitcast.18, ...), custom_call_target="tpu_custom_call", output_to_operand_aliasing={{0}: (2, {})} | custom-call | flops 339738624 | bytes 3833856 | tf_op jit(solution)/shard_map/depth_inverse/pallas_call | solution.py:215
  293.2 3.3 %collective-permute-start = (f32[1,2,4608]{2,1,0:T(2,128)}, f32[1,2,4608]{2,1,0:T(2,128)S(1)}, u32[]{:S(2)}, u32[]{:S(2)}) collective-permute-start(f32[1,2,4608]{2,1,0:T(2,128)} %get-tuple-element.21), channel_id=1, source_target_pairs={{0,8},{8,16},{16,24},{1,9},{9,17},{17,25},{2,10},{10,18},{18,26},{... | collective-permute-start | bytes 110600 | tf_op jit(solution)/shard_map/ppermute | solution.py:426
  296.6 1.3 collective-permute-start.1
  298.6 13.4 %stretch.2.refs_0_ = f32[3,48,4608]{2,1,0:T(8,128)} custom-call(f32[3,48,4608]{2,1,0:T(8,128)} %field_ref.3, f32[2,48,4608]{2,1,0:T(8,128)} %get-tuple-element.25.flow_ref, f32[2,2,4608]{2,1,0:T(2,128)} %copy-done.18, f32[2,2,4608]{2,1,0:T(2,128)} %copy-done.20, f32[2,48,384]{2,1,0:T(8,128)} %copy-done.16, f32[2,48,384]{2,1,0:T(8,128)} %copy-done.17, ...), custom_call_target="tpu_custom_call" | custom-call | flops 26542080 | bytes 6193152 | tf_op jit(solution)/shard_map/stretch/pallas_call | solution.py:513
  312.7 8.1 %stretch.3 = f32[3,48,4608]{2,1,0:T(8,128)} custom-call(f32[3,48,4608]{2,1,0:T(8,128)} %field_ref.3, f32[1,48,4608]{2,1,0:T(8,128)} %get-tuple-element.20.flow_ref, f32[1,2,4608]{2,1,0:T(2,128)} %copy-done.22, f32[1,2,4608]{2,1,0:T(2,128)} %copy-done.23, f32[1,48,384]{2,1,0:T(8,128)} %copy-done.19, ...), custom_call_target="tpu_custom_call", output_to_operand_aliasing={{}: (7, {})} | custom-call | flops 13271040 | bytes 4423680 | tf_op jit(solution)/shard_map/stretch/pallas_call | solution.py:513
  (60 shorter events, 18.6 us)
Async XLA Ops:
  7.4 50.4 %all-to-all-start.3 = ((f32[32,112,128]{2,1,0:T(8,128)}), f32[32,112,128]{2,1,0:T(8,128)S(1)}, u32[]{:S(2)}, u32[]{:S(2)}) async-start(f32[32,112,128]{2,1,0:T(8,128)} %bitcast.17), calls=%async_computation.3 | async-start | bytes 3670016 | tf_op jit(solution)/shard_map/all_to_all | solution.py:584
  57.9 1.2 copy-start.1
  59.1 4.2 %copy-start.14 = (f32[8,384]{1,0:T(8,128)S(1)}, f32[8,384]{1,0:T(8,128)}, u32[]{:S(2)}) copy-start(f32[8,384]{1,0:T(8,128)} %constant.41.clone.ky_ref) | copy-start | bytes 36868
  59.1 83.9 %all-to-all-start = ((f32[32,216,128]{2,1,0:T(8,128)}), f32[32,216,128]{2,1,0:T(8,128)S(1)}, u32[]{:S(2)}, u32[]{:S(2)}) async-start(f32[32,216,128]{2,1,0:T(8,128)} %bitcast.15), calls=%async_computation | async-start | bytes 7077888 | tf_op jit(solution)/shard_map/all_to_all | solution.py:584
  63.3 1.5 copy-start.2
  64.8 1.0 copy-start.4
  65.8 1.0 copy-start.6
  66.8 1.0 copy-start.8
  90.2 1.2 copy-start.3
  142.9 48.6 %all-to-all-start.4 = ((f32[32,112,128]{2,1,0:T(8,128)}), f32[32,112,128]{2,1,0:T(8,128)}, u32[]{:S(2)}, u32[]{:S(2)}) async-start(f32[32,112,128]{2,1,0:T(8,128)} %bitcast.14), calls=%async_computation.4 | async-start | bytes 3670016 | tf_op jit(solution)/shard_map/all_to_all | solution.py:584
  147.2 1.0 copy-start.5
  190.2 1.4 copy-start
  253.1 31.8 %all-to-all-start.1 = ((f32[32,72,128]{2,1,0:T(8,128)}), f32[32,72,128]{2,1,0:T(8,128)S(1)}, u32[]{:S(2)}, u32[]{:S(2)}) async-start(f32[32,72,128]{2,1,0:T(8,128)} %bitcast.3), calls=%async_computation.1 | async-start | bytes 2359296 | tf_op jit(solution)/shard_map/all_to_all | solution.py:584
  270.6 26.0 %collective-permute-start.6 = (f32[2,48,384]{2,1,0:T(8,128)}, f32[2,48,384]{2,1,0:T(8,128)S(1)}, u32[]{:S(2)}, u32[]{:S(2)}) collective-permute-start(f32[2,48,384]{2,1,0:T(8,128)} %get-tuple-element.28), channel_id=1, source_target_pairs={{0,1},{1,2},{2,3},{3,4},{4,5},{5,6},{6,7},{8,9},{9,10},{10,11},{11... | collective-permute-start | bytes 442376 | tf_op jit(solution)/shard_map/ppermute | solution.py:426
  272.4 25.5 %collective-permute-start.7 = (f32[2,48,384]{2,1,0:T(8,128)}, f32[2,48,384]{2,1,0:T(8,128)S(1)}, u32[]{:S(2)}, u32[]{:S(2)}) collective-permute-start(f32[2,48,384]{2,1,0:T(8,128)} %get-tuple-element.29), channel_id=1, source_target_pairs={{1,0},{2,1},{3,2},{4,3},{5,4},{6,5},{7,6},{9,8},{10,9},{11,10},{12... | collective-permute-start | bytes 442376 | tf_op jit(solution)/shard_map/ppermute | solution.py:426
  273.7 18.2 %collective-permute-start.4 = (f32[2,2,4608]{2,1,0:T(2,128)}, f32[2,2,4608]{2,1,0:T(2,128)S(1)}, u32[]{:S(2)}, u32[]{:S(2)}) collective-permute-start(f32[2,2,4608]{2,1,0:T(2,128)} %get-tuple-element.26), channel_id=1, source_target_pairs={{0,8},{8,16},{16,24},{1,9},{9,17},{17,25},{2,10},{10,18},{18,26},{... | collective-permute-start | bytes 221192 | tf_op jit(solution)/shard_map/ppermute | solution.py:426
  277.3 15.9 %collective-permute-start.5 = (f32[2,2,4608]{2,1,0:T(2,128)}, f32[2,2,4608]{2,1,0:T(2,128)S(1)}, u32[]{:S(2)}, u32[]{:S(2)}) collective-permute-start(f32[2,2,4608]{2,1,0:T(2,128)} %get-tuple-element.27), channel_id=1, source_target_pairs={{8,0},{16,8},{24,16},{9,1},{17,9},{25,17},{10,2},{18,10},{26,18},{... | collective-permute-start | bytes 221192 | tf_op jit(solution)/shard_map/ppermute | solution.py:426
  290.6 21.4 %collective-permute-start.2 = (f32[1,48,384]{2,1,0:T(8,128)}, f32[1,48,384]{2,1,0:T(8,128)S(1)}, u32[]{:S(2)}, u32[]{:S(2)}) collective-permute-start(f32[1,48,384]{2,1,0:T(8,128)} %get-tuple-element.23), channel_id=1, source_target_pairs={{0,1},{1,2},{2,3},{3,4},{4,5},{5,6},{6,7},{8,9},{9,10},{10,11},{11... | collective-permute-start | bytes 221192 | tf_op jit(solution)/shard_map/ppermute | solution.py:426
  291.9 6.0 %copy-start.18 = (f32[2,2,4608]{2,1,0:T(2,128)}, f32[2,2,4608]{2,1,0:T(2,128)S(1)}, u32[]{:S(2)}) copy-start(f32[2,2,4608]{2,1,0:T(2,128)S(1)} %collective-permute-done.4.up_ref) | copy-start | bytes 221188
  291.9 20.1 %collective-permute-start.3 = (f32[1,48,384]{2,1,0:T(8,128)}, f32[1,48,384]{2,1,0:T(8,128)S(1)}, u32[]{:S(2)}, u32[]{:S(2)}) collective-permute-start(f32[1,48,384]{2,1,0:T(8,128)} %get-tuple-element.24), channel_id=1, source_target_pairs={{1,0},{2,1},{3,2},{4,3},{5,4},{6,5},{7,6},{9,8},{10,9},{11,10},{12... | collective-permute-start | bytes 221192 | tf_op jit(solution)/shard_map/ppermute | solution.py:426
  293.2 4.7 %copy-start.20 = (f32[2,2,4608]{2,1,0:T(2,128)}, f32[2,2,4608]{2,1,0:T(2,128)S(1)}, u32[]{:S(2)}) copy-start(f32[2,2,4608]{2,1,0:T(2,128)S(1)} %collective-permute-done.5.down_ref) | copy-start | bytes 221188
  293.2 18.7 %collective-permute-start = (f32[1,2,4608]{2,1,0:T(2,128)}, f32[1,2,4608]{2,1,0:T(2,128)S(1)}, u32[]{:S(2)}, u32[]{:S(2)}) collective-permute-start(f32[1,2,4608]{2,1,0:T(2,128)} %get-tuple-element.21), channel_id=1, source_target_pairs={{0,8},{8,16},{16,24},{1,9},{9,17},{17,25},{2,10},{10,18},{18,26},{... | collective-permute-start | bytes 110600 | tf_op jit(solution)/shard_map/ppermute | solution.py:426
  296.6 1.4 copy-start.16
  296.6 15.4 %collective-permute-start.1 = (f32[1,2,4608]{2,1,0:T(2,128)}, f32[1,2,4608]{2,1,0:T(2,128)S(1)}, u32[]{:S(2)}, u32[]{:S(2)}) collective-permute-start(f32[1,2,4608]{2,1,0:T(2,128)} %get-tuple-element.22), channel_id=1, source_target_pairs={{8,0},{16,8},{24,16},{9,1},{17,9},{25,17},{10,2},{18,10},{26,18},{... | collective-permute-start | bytes 110600 | tf_op jit(solution)/shard_map/ppermute | solution.py:426
  (12 other events, 9.9 us)

commit v4 on v3

--- a/solution.py
+++ b/solution.py
@@ -15,6 +15,7 @@
 bf16 = jnp.bfloat16
 LANES = 128
 SUB = 8
+ROWS = 16
 PLANES_VMEM = 44 * 1024 * 1024
 
 
@@ -437,12 +438,13 @@
 def depth_weights(G):
     width = 2 * G
     at = np.arange(width) % G
-    out = np.zeros((width // LANES * 4, LANES), np.float32)
-    for i, (shift, weight) in enumerate(((1, 8.0), (-1, -8.0), (2, -1.0), (-2, 1.0))):
-        row = np.where((at + shift >= 0) & (at + shift < G), weight / 12.0, 0.0)
-        for k in range(width // LANES):
-            out[4 * k + i] = row[k * LANES : (k + 1) * LANES]
-    return out
+    rows = []
+    for k in range(width // LANES):
+        for shift, weight in ((1, 8.0), (-1, -8.0), (2, -1.0), (-2, 1.0)):
+            inside = (at + shift >= 0) & (at + shift < G)
+            rows.append(np.where(inside, weight / 12.0, 0.0)[k * LANES : (k + 1) * LANES])
+    rows = np.stack(rows).astype(np.float32)
+    return np.broadcast_to(rows[:, None, :], (len(rows), ROWS, LANES))
 
 
 def stretch(field, flow, halos, before, size, parts):
@@ -454,55 +456,57 @@
     extra = [] if before is None else [before]
 
     def kernel(field_ref, flow_ref, up_ref, down_ref, left_ref, right_ref, weight_ref, *refs):
-        out_ref, ext_ref, mix_ref = refs[len(extra) :]
+        out_ref, ext_ref, turned_ref = refs[len(extra) :]
+
+        def put(t, value):
+            ext_ref[t, SUB : SUB + rows, :] = value
+            turned_ref[t] = pltpu.roll(value, half, 1)
+
         for t in range(many):
             at = slice(t * LANES, (t + 1) * LANES)
-            ext_ref[span + t, SUB : SUB + rows, :] = flow_ref[0, :, at]
+            put(span + t, flow_ref[0, :, at])
             ext_ref[span + t, SUB - 2 : SUB, :] = up_ref[0, :, at]
             ext_ref[span + t, SUB + rows : SUB + rows + 2, :] = down_ref[0, :, at]
         for t in range(span):
             at = slice(t * LANES, (t + 1) * LANES)
-            ext_ref[t, SUB : SUB + rows, :] = left_ref[0, :, at]
-            ext_ref[span + many + t, SUB : SUB + rows, :] = right_ref[0, :, at]
-        lane = lax.broadcasted_iota(jnp.int32, (rows, LANES), 1)
-
-        def mix(t, turned):
-            after = pltpu.roll(ext_ref[t + 1, SUB : SUB + rows, :], half, 1)
-            mix_ref[t] = jnp.where(lane < half, turned, after)
-            return after
-
-        lax.fori_loop(
-            0, many + 2 * span - 1, mix, pltpu.roll(ext_ref[0, SUB : SUB + rows, :], half, 1)
-        )
+            put(t, left_ref[0, :, at])
+            put(span + many + t, right_ref[0, :, at])
+        lane = lax.broadcasted_iota(jnp.int32, (ROWS, LANES), 1)
 
         def block(b, _):
             base = span * (b + 1)
-            own = [ext_ref[base + k, SUB : SUB + rows, :] for k in range(span)]
-            moved = {
-                (k, s): pltpu.roll(own[k], (-s) % LANES, 1)
-                for k in range(span)
-                for s in (1, -1, 2, -2)
-            }
-            for k in range(span):
-                deep = 0.0
-                for i, s in enumerate((1, -1, 2, -2)):
-                    value = moved[k, s]
-                    if s > 0 and k + 1 < span:
-                        value = jnp.where(lane < LANES - s, value, moved[k + 1, s])
-                    if s < 0 and k > 0:
-                        value = jnp.where(lane >= -s, value, moved[k - 1, s])
-                    deep = deep + weight_ref[4 * k + i : 4 * k + i + 1, :] * value
-                t = base + k
-                side = 8.0 * (mix_ref[t + 1] - mix_ref[t - 2]) - (
-                    ext_ref[t + span, SUB : SUB + rows, :] - ext_ref[t - span, SUB : SUB + rows, :]
-                )
-                tall = 8.0 * (
-                    ext_ref[t, SUB + 1 : SUB + 1 + rows, :] - ext_ref[t, SUB - 1 : SUB - 1 + rows, :]
-                ) - (ext_ref[t, SUB + 2 : SUB + 2 + rows, :] - ext_ref[t, SUB - 2 : SUB - 2 + rows, :])
-                at = pl.ds(pl.multiple_of((span * b + k) * LANES, LANES), LANES)
-                out_ref[0, :, at] = field_ref[2, :, at] * deep + (1.0 / 12.0) * (
-                    field_ref[1, :, at] * side + field_ref[0, :, at] * tall
-                )
+            for top in range(0, rows, ROWS):
+                these = slice(top, top + ROWS)
+
+                def tall_at(t, s):
+                    return ext_ref[t, SUB + top + s : SUB + top + s + ROWS, :]
+
+                def side_at(t):
+                    return jnp.where(lane < half, turned_ref[t, these, :], turned_ref[t + 1, these, :])
+
+                own = [tall_at(base + k, 0) for k in range(span)]
+                for k in range(span):
+                    t = base + k
+                    deep = 0.0
+                    for i, s in enumerate((1, -1, 2, -2)):
+                        value = pltpu.roll(own[k], (-s) % LANES, 1)
+                        if s > 0 and k + 1 < span:
+                            value = jnp.where(
+                                lane < LANES - s, value, pltpu.roll(own[k + 1], (-s) % LANES, 1)
+                            )
+                        if s < 0 and k > 0:
+                            value = jnp.where(
+                                lane >= -s, value, pltpu.roll(own[k - 1], (-s) % LANES, 1)
+                            )
+                        deep = deep + weight_ref[4 * k + i] * value
+                    side = 8.0 * (side_at(t + 1) - side_at(t - 2)) - (
+                        tall_at(t + span, 0) - tall_at(t - span, 0)
+                    )
+                    tall = 8.0 * (tall_at(t, 1) - tall_at(t, -1)) - (tall_at(t, 2) - tall_at(t, -2))
+                    at = pl.ds(pl.multiple_of((span * b + k) * LANES, LANES), LANES)
+                    out_ref[0, these, at] = field_ref[2, these, at] * deep + (1.0 / 12.0) * (
+                        field_ref[1, these, at] * side + field_ref[0, these, at] * tall
+                    )
             return 0
 
         lax.fori_loop(0, cols // 2, block, 0)
@@ -521,14 +525,14 @@
             part(2, cols * G),
             part(rows, 2 * G),
             part(rows, 2 * G),
-            pl.BlockSpec((4 * span, LANES), lambda i: (0, 0)),
+            pl.BlockSpec((4 * span, ROWS, LANES), lambda i: (0, 0, 0)),
         ]
         + [pl.BlockSpec(memory_space=pl.ANY)] * len(extra),
         out_specs=pl.BlockSpec((1, rows, cols * G), lambda i: (start + i, 0, 0)),
         input_output_aliases={7: 0} if extra else {},
         scratch_shapes=[
             pltpu.VMEM((many + 2 * span, rows + 2 * SUB, LANES), f32),
-            pltpu.VMEM((many + 2 * span - 1, rows, LANES), f32),
+            pltpu.VMEM((many + 2 * span, rows, LANES), f32),
         ],
         cost_estimate=pl.CostEstimate(
             flops=60 * flow.size,

time: 324 us -> 316 us (0.975)
  Pallas kernels: 115 us -> 106 us
    pallas_call x2, Pallas kernels: 21.5 us -> 13 us  [stretch(): pl.pallas_call(kernel, grid=(count,), out_shape=jax.ShapeDtypeStruct((3,...]
    unnamed x48 -> x50, local copies, waits for them, and re-layouts: 17.5 us -> 16.8 us
  transfers between devices with their start and end apart: 12 -> 12, of which waited for: 3 -> 3; matrix products, arithmetic and copies ran while one was open for 0% -> 0% of each run, Pallas kernels for 31% -> 30%
where the time goes in v4:
time: 316 us; the launch traced here: 312 us
  Pallas kernels  106 us (34%)
  waiting for transfers between devices  92 us (29%)
  blocking collectives  61.6 us (19%)
  starting transfers between devices  33.8 us (11%)
  local copies, waits for them, and re-layouts  17.5 us (6%)
    all_to_all x4, waiting for transfers between devices, exchange(): return lax.all_to_all(value, axes, split_axis=0, concat_axis=0, tiled=True)  92 us
    all_to_all x1, blocking collectives, exchange(): return lax.all_to_all(value, axes, split_axis=0, concat_axis=0, tiled=True)  61.6 us
    pallas_call x2, Pallas kernels, planes(): pl.pallas_call(kernel, out_shape=[jax.ShapeDtypeStruct((groups, others, s...  58.6 us
    pallas_call x3, Pallas kernels, depth_inverse(): pl.pallas_call(kernel, grid=(1,), out_shape=outs, in_specs=[whole, whole]...  19.3 us
    all_to_all x4, starting transfers between devices, exchange(): return lax.all_to_all(value, axes, split_axis=0, concat_axis=0, tiled=True)  18.5 us
    unnamed x50, local copies, waits for them, and re-layouts  16.8 us
    pallas_call x2, Pallas kernels, depth_forward(): pl.pallas_call(kernel, out_shape=jax.ShapeDtypeStruct((devices * tiles *...  15.5 us
    ppermute x8, starting transfers between devices, shifted(): return lax.ppermute(piece, axis, pairs)  15.4 us
  transfers between devices with their start and end apart: 12, of which 3 were waited for; matrix products, arithmetic and copies ran while one was open for 0% of the time, Pallas kernels for 30%

profile of v4, /device:TPU:0, one launch (start us, length us, event | category | flops | bytes accessed | tf_op | source)
XLA Modules:
  0.0 312.3 jit_solution(17847228341852434226)
XLA Ops:
  0.6 6.8 %depth_forward.3 = f32[3584,128]{1,0:T(8,128)} custom-call(f32[3,48,4608]{2,1,0:T(8,128)} %field_ref.3, bf16[2,128,192]{2,1,0:T(8,128)(2,1)} %constant.42.clone.table_ref), custom_call_target="tpu_custom_call" | custom-call | flops 509607936 | bytes 4489216 | tf_op jit(solution)/shard_map/depth_forward/pallas_call | solution.py:135
  7.4 7.3 %all-to-all-start.3 = ((f32[32,112,128]{2,1,0:T(8,128)}), f32[32,112,128]{2,1,0:T(8,128)S(1)}, u32[]{:S(2)}, u32[]{:S(2)}) async-start(f32[32,112,128]{2,1,0:T(8,128)} %bitcast.17), calls=%async_computation.3 | async-start | bytes 3670016 | tf_op jit(solution)/shard_map/all_to_all | solution.py:588
  14.8 8.7 %depth_forward.2 = f32[6912,128]{1,0:T(8,128)} custom-call(f32[3,48,4608]{2,1,0:T(8,128)} %field_ref.3, bf16[2,256,192]{2,1,0:T(8,128)(2,1)} %constant.43.clone.table_ref), custom_call_target="tpu_custom_call" | custom-call | flops 1019215872 | bytes 6193152 | tf_op jit(solution)/shard_map/depth_forward/pallas_call | solution.py:135
  23.4 34.4 %all-to-all-done.3 = f32[32,112,128]{2,1,0:T(8,128)S(1)} async-done(((f32[32,112,128]{2,1,0:T(8,128)}), f32[32,112,128]{2,1,0:T(8,128)S(1)}, u32[]{:S(2)}, u32[]{:S(2)}) %all-to-all-start.3) | async-done | bytes 1835040 | tf_op jit(solution)/shard_map/all_to_all | solution.py:588
  59.1 4.1 %all-to-all-start = ((f32[32,216,128]{2,1,0:T(8,128)}), f32[32,216,128]{2,1,0:T(8,128)S(1)}, u32[]{:S(2)}, u32[]{:S(2)}) async-start(f32[32,216,128]{2,1,0:T(8,128)} %bitcast.15), calls=%async_computation | async-start | bytes 7077888 | tf_op jit(solution)/shard_map/all_to_all | solution.py:588
  63.3 1.5 copy-done.2
  69.7 20.5 %planes.3 = f32[4,8,14,8,128]{4,3,2,1,0:T(8,128)S(1)} custom-call(s32[2]{0:T(128)S(1)} %pad_add_fusion.1.place_ref, f32[4,8,14,8,128]{4,3,2,1,0:T(8,128)S(1)} %bitcast.13, bf16[2,192,384]{2,1,0:T(8,128)(2,1)S(1)} %copy-done.10, bf16[384,576]{1,0:T(8,128)(2,1)S(1)} %copy-done.4, bf16[192,1152]{1,0:T(8,128)(2,1)S(1)} %copy-done.6, ...), custom_call_target="tpu_custom_call" | custom-call | flops 12230590464 | bytes 3670016 | tf_op jit(solution)/shard_map/planes/pallas_call | solution.py:399
  91.5 51.5 %all-to-all-done = f32[32,216,128]{2,1,0:T(8,128)S(1)} async-done(((f32[32,216,128]{2,1,0:T(8,128)}), f32[32,216,128]{2,1,0:T(8,128)S(1)}, u32[]{:S(2)}, u32[]{:S(2)}) %all-to-all-start) | async-done | bytes 3538976 | tf_op jit(solution)/shard_map/all_to_all | solution.py:588
  142.9 4.2 %all-to-all-start.4 = ((f32[32,112,128]{2,1,0:T(8,128)}), f32[32,112,128]{2,1,0:T(8,128)}, u32[]{:S(2)}, u32[]{:S(2)}) async-start(f32[32,112,128]{2,1,0:T(8,128)} %bitcast.14), calls=%async_computation.4 | async-start | bytes 3670016 | tf_op jit(solution)/shard_map/all_to_all | solution.py:588
  152.1 38.0 %planes.2 = (f32[4,8,18,8,128]{4,3,2,1,0:T(8,128)S(1)}, f32[4,8,9,8,128]{4,3,2,1,0:T(8,128)}) custom-call(s32[2]{0:T(128)S(1)} %pad_add_fusion.place_ref, f32[4,8,27,8,128]{4,3,2,1,0:T(8,128)S(1)} %bitcast.11, bf16[2,192,384]{2,1,0:T(8,128)(2,1)S(1)} %copy-done.11, bf16[384,576]{1,0:T(8,128)(2,1)S(1)} %copy-done.5, bf16[192,1152]{1,0:T(8,128)(2,1)S(1)} %copy-done.7, ...), custom_call_target="tpu_custom_call" | custom-call | flops 24461180928 | bytes 7077888 | tf_op jit(solution)/shard_map/planes/pallas_call | solution.py:399
  190.2 1.4 copy-done
  191.6 61.6 %all_to_all.25 = f32[32,144,128]{2,1,0:T(8,128)} all-to-all(f32[32,144,128]{2,1,0:T(8,128)} %bitcast.12), channel_id=1, replica_groups=mesh['px'=4,'py'=8] {'px','py'}, dimensions={0} | all-to-all | bytes 4718592 | tf_op jit(solution)/shard_map/all_to_all | solution.py:588
  253.1 2.8 all-to-all-start.1
  256.0 6.8 %depth_inverse.3.refs_0_ = f32[3,48,4608]{2,1,0:T(8,128)} custom-call(f32[3584,128]{1,0:T(8,128)} %bitcast.10.lines_ref, bf16[2,128,192]{2,1,0:T(8,128)(2,1)} %constant.44.clone.table_ref), custom_call_target="tpu_custom_call" | custom-call | flops 509607936 | bytes 9797632 | tf_op jit(solution)/shard_map/depth_inverse/pallas_call | solution.py:216
  262.8 7.8 %depth_inverse.4 = (f32[3,48,4608]{2,1,0:T(8,128)}, f32[2,2,4608]{2,1,0:T(2,128)}, f32[2,2,4608]{2,1,0:T(2,128)}, f32[2,48,384]{2,1,0:T(8,128)}, f32[2,48,384]{2,1,0:T(8,128)}, /*index=5*/f32[2,48,4608]{2,1,0:T(8,128)}) custom-call(f32[4608,128]{1,0:T(8,128)} %bitcast.16, ...), custom_call_target="tpu_custom_call", output_to_operand_aliasing={{0}: (2, {})} | custom-call | flops 679477248 | bytes 7667712 | tf_op jit(solution)/shard_map/depth_inverse/pallas_call | solution.py:216
  270.6 2.0 collective-permute-start.6
  272.6 1.3 collective-permute-start.7
  273.9 3.6 %collective-permute-start.4 = (f32[2,2,4608]{2,1,0:T(2,128)}, f32[2,2,4608]{2,1,0:T(2,128)S(1)}, u32[]{:S(2)}, u32[]{:S(2)}) collective-permute-start(f32[2,2,4608]{2,1,0:T(2,128)} %get-tuple-element.26), channel_id=1, source_target_pairs={{0,8},{8,16},{16,24},{1,9},{9,17},{17,25},{2,10},{10,18},{18,26},{... | collective-permute-start | bytes 221192 | tf_op jit(solution)/shard_map/ppermute | solution.py:427
  277.5 1.3 collective-permute-start.5
  278.8 6.1 %all-to-all-done.1 = f32[32,72,128]{2,1,0:T(8,128)S(1)} async-done(((f32[32,72,128]{2,1,0:T(8,128)}), f32[32,72,128]{2,1,0:T(8,128)S(1)}, u32[]{:S(2)}, u32[]{:S(2)}) %all-to-all-start.1) | async-done | bytes 1179680 | tf_op jit(solution)/shard_map/all_to_all | solution.py:588
  285.9 4.7 %depth_inverse.5 = (f32[3,48,4608]{2,1,0:T(8,128)}, f32[1,2,4608]{2,1,0:T(2,128)}, f32[1,2,4608]{2,1,0:T(2,128)}, f32[1,48,384]{2,1,0:T(8,128)}, f32[1,48,384]{2,1,0:T(8,128)}, /*index=5*/f32[1,48,4608]{2,1,0:T(8,128)}) custom-call(f32[2304,128]{1,0:T(8,128)} %bitcast.18, ...), custom_call_target="tpu_custom_call", output_to_operand_aliasing={{0}: (2, {})} | custom-call | flops 339738624 | bytes 3833856 | tf_op jit(solution)/shard_map/depth_inverse/pallas_call | solution.py:216
  293.2 3.3 %collective-permute-start = (f32[1,2,4608]{2,1,0:T(2,128)}, f32[1,2,4608]{2,1,0:T(2,128)S(1)}, u32[]{:S(2)}, u32[]{:S(2)}) collective-permute-start(f32[1,2,4608]{2,1,0:T(2,128)} %get-tuple-element.21), channel_id=1, source_target_pairs={{0,8},{8,16},{16,24},{1,9},{9,17},{17,25},{2,10},{10,18},{18,26},{... | collective-permute-start | bytes 110600 | tf_op jit(solution)/shard_map/ppermute | solution.py:427
  298.6 7.8 %stretch.2.refs_0_ = f32[3,48,4608]{2,1,0:T(8,128)} custom-call(f32[3,48,4608]{2,1,0:T(8,128)} %field_ref.3, f32[2,48,4608]{2,1,0:T(8,128)} %get-tuple-element.25.flow_ref, f32[2,2,4608]{2,1,0:T(2,128)} %copy-done.18, f32[2,2,4608]{2,1,0:T(2,128)} %copy-done.19, f32[2,48,384]{2,1,0:T(8,128)} %copy-done.16, f32[2,48,384]{2,1,0:T(8,128)} %copy-done.17, ...), custom_call_target="tpu_custom_call" | custom-call | flops 26542080 | bytes 6193152 | tf_op jit(solution)/shard_map/stretch/pallas_call | solution.py:517
  307.1 5.3 %stretch.3 = f32[3,48,4608]{2,1,0:T(8,128)} custom-call(f32[3,48,4608]{2,1,0:T(8,128)} %field_ref.3, f32[1,48,4608]{2,1,0:T(8,128)} %get-tuple-element.20.flow_ref, f32[1,2,4608]{2,1,0:T(2,128)} %copy-done.22, f32[1,2,4608]{2,1,0:T(2,128)} %copy-done.23, f32[1,48,384]{2,1,0:T(8,128)} %copy-done.20, ...), custom_call_target="tpu_custom_call", output_to_operand_aliasing={{}: (7, {})} | custom-call | flops 13271040 | bytes 4423680 | tf_op jit(solution)/shard_map/stretch/pallas_call | solution.py:517
  (63 shorter events, 18.6 us)
Async XLA Ops:
  7.4 50.4 %all-to-all-start.3 = ((f32[32,112,128]{2,1,0:T(8,128)}), f32[32,112,128]{2,1,0:T(8,128)S(1)}, u32[]{:S(2)}, u32[]{:S(2)}) async-start(f32[32,112,128]{2,1,0:T(8,128)} %bitcast.17), calls=%async_computation.3 | async-start | bytes 3670016 | tf_op jit(solution)/shard_map/all_to_all | solution.py:588
  57.9 1.2 copy-start.1
  59.1 4.2 %copy-start.14 = (f32[8,384]{1,0:T(8,128)S(1)}, f32[8,384]{1,0:T(8,128)}, u32[]{:S(2)}) copy-start(f32[8,384]{1,0:T(8,128)} %constant.41.clone.ky_ref) | copy-start | bytes 36868
  59.1 83.9 %all-to-all-start = ((f32[32,216,128]{2,1,0:T(8,128)}), f32[32,216,128]{2,1,0:T(8,128)S(1)}, u32[]{:S(2)}, u32[]{:S(2)}) async-start(f32[32,216,128]{2,1,0:T(8,128)} %bitcast.15), calls=%async_computation | async-start | bytes 7077888 | tf_op jit(solution)/shard_map/all_to_all | solution.py:588
  63.3 1.5 copy-start.2
  64.8 1.0 copy-start.4
  65.8 1.0 copy-start.6
  90.2 1.2 copy-start.3
  142.9 48.6 %all-to-all-start.4 = ((f32[32,112,128]{2,1,0:T(8,128)}), f32[32,112,128]{2,1,0:T(8,128)}, u32[]{:S(2)}, u32[]{:S(2)}) async-start(f32[32,112,128]{2,1,0:T(8,128)} %bitcast.14), calls=%async_computation.4 | async-start | bytes 3670016 | tf_op jit(solution)/shard_map/all_to_all | solution.py:588
  147.2 1.0 copy-start.5
  190.2 1.4 copy-start
  253.1 31.8 %all-to-all-start.1 = ((f32[32,72,128]{2,1,0:T(8,128)}), f32[32,72,128]{2,1,0:T(8,128)S(1)}, u32[]{:S(2)}, u32[]{:S(2)}) async-start(f32[32,72,128]{2,1,0:T(8,128)} %bitcast.3), calls=%async_computation.1 | async-start | bytes 2359296 | tf_op jit(solution)/shard_map/all_to_all | solution.py:588
  270.6 27.3 %copy-start.24 = (f32[12,128]{1,0:T(8,128)S(1)}, f32[12,128]{1,0:T(8,128)}, u32[]{:S(2)}) copy-start(f32[12,128]{1,0:T(8,128)} %constant.46.clone) | copy-start | bytes 18436
  270.6 26.0 %collective-permute-start.6 = (f32[2,48,384]{2,1,0:T(8,128)}, f32[2,48,384]{2,1,0:T(8,128)S(1)}, u32[]{:S(2)}, u32[]{:S(2)}) collective-permute-start(f32[2,48,384]{2,1,0:T(8,128)} %get-tuple-element.28), channel_id=1, source_target_pairs={{0,1},{1,2},{2,3},{3,4},{4,5},{5,6},{6,7},{8,9},{9,10},{10,11},{11... | collective-permute-start | bytes 442376 | tf_op jit(solution)/shard_map/ppermute | solution.py:427
  272.6 25.3 %collective-permute-start.7 = (f32[2,48,384]{2,1,0:T(8,128)}, f32[2,48,384]{2,1,0:T(8,128)S(1)}, u32[]{:S(2)}, u32[]{:S(2)}) collective-permute-start(f32[2,48,384]{2,1,0:T(8,128)} %get-tuple-element.29), channel_id=1, source_target_pairs={{1,0},{2,1},{3,2},{4,3},{5,4},{6,5},{7,6},{9,8},{10,9},{11,10},{12... | collective-permute-start | bytes 442376 | tf_op jit(solution)/shard_map/ppermute | solution.py:427
  273.9 18.0 %collective-permute-start.4 = (f32[2,2,4608]{2,1,0:T(2,128)}, f32[2,2,4608]{2,1,0:T(2,128)S(1)}, u32[]{:S(2)}, u32[]{:S(2)}) collective-permute-start(f32[2,2,4608]{2,1,0:T(2,128)} %get-tuple-element.26), channel_id=1, source_target_pairs={{0,8},{8,16},{16,24},{1,9},{9,17},{17,25},{2,10},{10,18},{18,26},{... | collective-permute-start | bytes 221192 | tf_op jit(solution)/shard_map/ppermute | solution.py:427
  277.5 15.7 %collective-permute-start.5 = (f32[2,2,4608]{2,1,0:T(2,128)}, f32[2,2,4608]{2,1,0:T(2,128)S(1)}, u32[]{:S(2)}, u32[]{:S(2)}) collective-permute-start(f32[2,2,4608]{2,1,0:T(2,128)} %get-tuple-element.27), channel_id=1, source_target_pairs={{8,0},{16,8},{24,16},{9,1},{17,9},{25,17},{10,2},{18,10},{26,18},{... | collective-permute-start | bytes 221192 | tf_op jit(solution)/shard_map/ppermute | solution.py:427
  290.6 15.8 %collective-permute-start.2 = (f32[1,48,384]{2,1,0:T(8,128)}, f32[1,48,384]{2,1,0:T(8,128)S(1)}, u32[]{:S(2)}, u32[]{:S(2)}) collective-permute-start(f32[1,48,384]{2,1,0:T(8,128)} %get-tuple-element.23), channel_id=1, source_target_pairs={{0,1},{1,2},{2,3},{3,4},{4,5},{5,6},{6,7},{8,9},{9,10},{10,11},{11... | collective-permute-start | bytes 221192 | tf_op jit(solution)/shard_map/ppermute | solution.py:427
  291.9 6.7 %copy-start.18 = (f32[2,2,4608]{2,1,0:T(2,128)}, f32[2,2,4608]{2,1,0:T(2,128)S(1)}, u32[]{:S(2)}) copy-start(f32[2,2,4608]{2,1,0:T(2,128)S(1)} %collective-permute-done.4.up_ref) | copy-start | bytes 221188
  291.9 14.5 %collective-permute-start.3 = (f32[1,48,384]{2,1,0:T(8,128)}, f32[1,48,384]{2,1,0:T(8,128)S(1)}, u32[]{:S(2)}, u32[]{:S(2)}) collective-permute-start(f32[1,48,384]{2,1,0:T(8,128)} %get-tuple-element.24), channel_id=1, source_target_pairs={{1,0},{2,1},{3,2},{4,3},{5,4},{6,5},{7,6},{9,8},{10,9},{11,10},{12... | collective-permute-start | bytes 221192 | tf_op jit(solution)/shard_map/ppermute | solution.py:427
  293.2 5.4 %copy-start.19 = (f32[2,2,4608]{2,1,0:T(2,128)}, f32[2,2,4608]{2,1,0:T(2,128)S(1)}, u32[]{:S(2)}) copy-start(f32[2,2,4608]{2,1,0:T(2,128)S(1)} %collective-permute-done.5.down_ref) | copy-start | bytes 221188
  293.2 13.2 %collective-permute-start = (f32[1,2,4608]{2,1,0:T(2,128)}, f32[1,2,4608]{2,1,0:T(2,128)S(1)}, u32[]{:S(2)}, u32[]{:S(2)}) collective-permute-start(f32[1,2,4608]{2,1,0:T(2,128)} %get-tuple-element.21), channel_id=1, source_target_pairs={{0,8},{8,16},{16,24},{1,9},{9,17},{17,25},{2,10},{10,18},{18,26},{... | collective-permute-start | bytes 110600 | tf_op jit(solution)/shard_map/ppermute | solution.py:427
  296.6 2.0 copy-start.16
  296.6 9.8 %collective-permute-start.1 = (f32[1,2,4608]{2,1,0:T(2,128)}, f32[1,2,4608]{2,1,0:T(2,128)S(1)}, u32[]{:S(2)}, u32[]{:S(2)}) collective-permute-start(f32[1,2,4608]{2,1,0:T(2,128)} %get-tuple-element.22), channel_id=1, source_target_pairs={{8,0},{16,8},{24,16},{9,1},{17,9},{25,17},{10,2},{18,10},{26,18},{... | collective-permute-start | bytes 110600 | tf_op jit(solution)/shard_map/ppermute | solution.py:427
  (13 other events, 11.0 us)
